TPU v7x, 512 devices: a whole 4x4x16 slice. The times are simulated.
512 devices in a mesh: span: 64 (over x, z_lo, y), col: 8 (over z_hi, core).
Axes of the slice: x: 4, y: 4, z: 16 (z_hi: 4, z_lo: 4; z = z_hi * 4 + z_lo), core: 2. Of those that a mesh axis runs over, the one named last changes fastest.
Arguments:
- adjoint_field: float32 [3, 512, 16, 1024], P(None, 'span', None, 'col'), may hold values from -6 to 6
- base_flow: float32 [3, 512, 16, 1024], P(None, 'span', None, 'col'), may hold values from -5 to 5
- metric_diag: bfloat16 [3, 512, 16, 1024], P(None, 'span', None, 'col'), may hold values from 1 to 2
- metric_cross: bfloat16 [3, 512, 16, 1024], P(None, 'span', None, 'col'), may hold values from -0.44921875 to 0.44921875
- jacobian: float32 [512, 16, 1024], P('span', None, 'col'), may hold values from 0.5 to 2
Outputs:
- advanced: float32 [3, 512, 16, 1024], P(None, 'span', None, 'col')
All inputs are finite; a program needn't handle non-finite values.
Results may differ from a plain program's by a relative error of at most 0.0003.
Values sent between devices are 32-bit elements; how exact they have to be, the bound alone decides.
A program may use at most 64 MiB of HBM per device.

v0:
```python
import jax
import jax.numpy as jnp
import numpy as np
from jax import lax
from jax.sharding import PartitionSpec as P

HIGH = lax.Precision.HIGHEST
VISCOSITY = 0.05
STEP_SIZE = 0.01
GLL_INNER = [
    -0.8717401485096066,
    -0.5917001814331423,
    -0.2092992179024789,
    0.2092992179024789,
    0.5917001814331423,
    0.8717401485096066,
]
GAUSS_POINTS = [
    -0.9815606342467192,
    -0.9041172563704749,
    -0.7699026741943047,
    -0.5873179542866175,
    -0.3678314989981802,
    -0.1252334085114689,
    0.1252334085114689,
    0.3678314989981802,
    0.5873179542866175,
    0.7699026741943047,
    0.9041172563704749,
    0.9815606342467192,
]
GAUSS_WEIGHTS = [
    0.0471753363865118,
    0.1069393259953184,
    0.1600783285433462,
    0.2031674267230659,
    0.2334925365383548,
    0.2491470458134028,
    0.2491470458134028,
    0.2334925365383548,
    0.2031674267230659,
    0.1600783285433462,
    0.1069393259953184,
    0.0471753363865118,
]


def padded_2(block, sides, width, periodic):
    for axis, dim in sides:
        count = lax.axis_size(axis)
        forward = [(i, i + 1) for i in range(count - 1)]
        if periodic:
            forward.append((count - 1, 0))
        backward = [(target, source) for source, target in forward]
        low = lax.ppermute(
            lax.slice_in_dim(block, block.shape[dim] - width, None, axis=dim), axis, forward
        )
        high = lax.ppermute(lax.slice_in_dim(block, 0, width, axis=dim), axis, backward)
        block = jnp.concatenate([low, block, high], axis=dim)
    return block


def legendre_seven(points):
    previous = points * 0.0 + 1.0
    current = points
    for degree in range(1, 7):
        following = ((2.0 * degree + 1.0) * points * current - degree * previous) / (degree + 1.0)
        previous = current
        current = following
    return current


def node_tables():
    gll_nodes = np.array([-1.0] + GLL_INNER + [1.0])
    values = legendre_seven(gll_nodes)
    node_weights = 2.0 / (56.0 * values * values)
    identity = np.eye(8, dtype=bool)
    spacing = gll_nodes[:, None] - gll_nodes[None, :]
    derivative = np.where(
        identity, 0.0, values[:, None] / (values[None, :] * np.where(identity, 1.0, spacing))
    )
    corner_terms = np.concatenate([np.array([-14.0]), np.zeros(6), np.array([14.0])])
    derivative = derivative + np.eye(8) * corner_terms[None, :]
    gauss_nodes = np.array(GAUSS_POINTS)
    gauss_weights = np.array(GAUSS_WEIGHTS)
    numerators = gauss_nodes[:, None, None] - gll_nodes[None, None, :]
    denominators = np.where(identity, 1.0, spacing)[None]
    ratios = np.where(identity[None], 1.0, numerators / denominators)
    interpolation = ratios.prod(axis=2)
    slope_interp = interpolation @ derivative
    return (derivative, node_weights, interpolation, slope_interp, gauss_weights)


def float_tables():
    return tuple((jnp.asarray(member, jnp.float32) for member in node_tables()))


def along_first(vector, matrix):
    leading, first_len, second_len, third_len = vector.shape
    columns = matrix.shape[1]
    blocks = vector.reshape(leading, first_len // columns, columns, second_len, third_len)
    result = jnp.einsum("pi,laimz->lapmz", matrix, blocks, precision=HIGH)
    return result.reshape(leading, -1, second_len, third_len)


def along_second(vector, matrix):
    leading, first_len, second_len, third_len = vector.shape
    columns = matrix.shape[1]
    blocks = vector.reshape(leading, first_len, second_len // columns, columns, third_len)
    result = jnp.einsum("pi,lxaiz->lxapz", matrix, blocks, precision=HIGH)
    return result.reshape(leading, first_len, -1, third_len)


def along_third(vector, matrix, group_size):
    leading, first_len, second_len, third_len = vector.shape
    columns = matrix.shape[1]
    kron_table = jnp.kron(jnp.eye(group_size, dtype=jnp.float32), matrix.T)
    blocks = vector.reshape(
        leading, first_len, second_len, third_len // (group_size * columns), group_size * columns
    )
    result = jnp.einsum("lxyzk,kq->lxyzq", blocks, kron_table, precision=HIGH)
    return result.reshape(leading, first_len, second_len, -1)


def interpolate(vector, matrix, group_size):
    return along_third(along_second(along_first(vector, matrix), matrix), matrix, group_size)


def weight_grid(weights, extent):
    nodes_per = weights.shape[0]
    first_axis = jnp.tile(weights, extent[0] // nodes_per)
    second_axis = jnp.tile(weights, extent[1] // nodes_per)
    third_axis = jnp.tile(weights, extent[2] // nodes_per)
    return first_axis[:, None, None] * second_axis[None, :, None] * third_axis[None, None, :]


def transposed_operator(vector, velocity_fine, metric_diag, metric_cross, group_size, tables):
    derivative, node_weights, interpolation, slope_interp, gauss_weights = tables
    grad_first = along_first(vector, derivative)
    grad_second = along_second(vector, derivative)
    grad_third = along_third(vector, derivative, group_size)
    scaled = VISCOSITY * weight_grid(node_weights, vector.shape[1:])
    flux_first = scaled * (
        metric_diag[0] * grad_first + metric_cross[0] * grad_second + metric_cross[1] * grad_third
    )
    flux_second = scaled * (
        metric_cross[0] * grad_first + metric_diag[1] * grad_second + metric_cross[2] * grad_third
    )
    flux_third = scaled * (
        metric_cross[1] * grad_first + metric_cross[2] * grad_second + metric_diag[2] * grad_third
    )
    stiffness = (
        along_first(flux_first, derivative.T)
        + along_second(flux_second, derivative.T)
        + along_third(flux_third, derivative.T, group_size)
    )
    fine_field = interpolate(vector, interpolation, group_size)
    weighted = fine_field * weight_grid(gauss_weights, fine_field.shape[1:])
    back_first = along_first(
        along_second(
            along_third(velocity_fine[0] * weighted, interpolation.T, group_size), interpolation.T
        ),
        slope_interp.T,
    )
    back_second = along_first(
        along_second(
            along_third(velocity_fine[1] * weighted, interpolation.T, group_size), slope_interp.T
        ),
        interpolation.T,
    )
    back_third = along_first(
        along_second(
            along_third(velocity_fine[2] * weighted, slope_interp.T, group_size), interpolation.T
        ),
        interpolation.T,
    )
    return stiffness + back_first + back_second + back_third


def add_partners(padded, which_axis):
    nodes_along = padded.shape[which_axis] - 2
    middle_part = lax.slice_in_dim(padded, 1, nodes_along + 1, axis=which_axis)
    next_part = lax.slice_in_dim(padded, 2, nodes_along + 2, axis=which_axis)
    before = lax.slice_in_dim(padded, 0, nodes_along, axis=which_axis)
    position = (jnp.arange(nodes_along) % 8).reshape(
        tuple((nodes_along if dimension == which_axis else 1 for dimension in range(padded.ndim)))
    )
    return (
        middle_part
        + jnp.where(position == 7, next_part, 0.0)
        + jnp.where(position == 0, before, 0.0)
    )


def wrap_second(vector):
    return add_partners(jnp.concatenate([vector[:, :, -1:], vector, vector[:, :, :1]], axis=2), 2)


def assemble(vector):
    streamwise = add_partners(padded_2(vector, (("span", 1),), 1, True), 1)
    summed = add_partners(padded_2(streamwise, (("col", 3),), 1, False), 3)
    return wrap_second(summed)


def local(adjoint_field, base_flow, metric_diag, metric_cross, jacobian):
    tables = float_tables()
    planes = jacobian.shape[2]
    group_size = min(planes // 8, 16)
    velocity_fine = interpolate(base_flow, tables[2], group_size)
    first_term = transposed_operator(
        adjoint_field, velocity_fine, metric_diag, metric_cross, group_size, tables
    )
    mass_terms = jacobian * weight_grid(tables[1], jacobian.shape)
    assembled = assemble(jnp.concatenate([first_term, mass_terms[None]], axis=0))
    inverse_mass = 1.0 / assembled[3]
    total_planes = planes * lax.axis_size("col")
    global_plane = lax.axis_index("col") * planes + jnp.arange(planes)
    interior = ((global_plane > 0) & (global_plane < total_planes - 1)).astype(jnp.float32)
    half_state = interior * (adjoint_field - 0.5 * STEP_SIZE * inverse_mass * assembled[:3])
    second_term = assemble(
        transposed_operator(
            half_state, velocity_fine, metric_diag, metric_cross, group_size, tables
        )
    )
    return interior * (adjoint_field - STEP_SIZE * inverse_mass * second_term)


def solution(mesh):
    in_specs = (
        P(None, "span", None, "col"),
        P(None, "span", None, "col"),
        P(None, "span", None, "col"),
        P(None, "span", None, "col"),
        P("span", None, "col"),
    )
    out_specs = P(None, "span", None, "col")
    return jax.shard_map(local, mesh=mesh, in_specs=in_specs, out_specs=out_specs, check_vma=False)
```

profile of v0, /device:TPU:1, one launch (start us, length us, event | category | flops | bytes accessed | tf_op | source)
XLA Modules:
  0.0 125.0 jit_solution(9417300104283069617)
XLA Ops:
  0.0 0.7 tile.8
  0.8 0.7 tile.10
  1.6 1.3 %broadcast_multiply_fusion.12 = f32[12,24]{1,0:T(8,128)} fusion(f32[24]{0:T(128)S(1)} %mul.721, f32[12]{0:T(128)} %constant.82.clone), kind=kLoop, calls=%fused_computation.198 | loop fusion | flops 288 | bytes 1296 | tf_op jit(solution)/shard_map/mul | solution.py:134
  2.9 0.7 broadcast_multiply_fusion.13
  3.7 0.7 tile.9
  4.4 0.7 tile.11
  5.2 1.3 %convolution_bitcast_fusion.23 = f32[3,8,16,128]{3,1,2,0:T(8,128)S(1)} fusion(f32[8,8,1,1]{1,0,3,2:T(8,128)} %constant.90, f32[3,8,16,128]{3,2,1,0:T(8,128)} %param.10), kind=kOutput, calls=%fused_computation.35 | convolution fusion | flops 4718592 | bytes 393472 | tf_op jit(solution)/shard_map/pi,laimz->lapmz/dot_general | solution.py:102
  6.5 1.4 %convolution_bitcast_fusion.22 = f32[3,8,2,8,128]{4,3,2,1,0:T(8,128)S(1)} fusion(f32[8,8,1,1,1]{1,0,4,3,2:T(8,128)} %constant.91, f32[3,8,16,128]{3,2,1,0:T(8,128)} %param.10), kind=kOutput, calls=%fused_computation.34 | convolution fusion | flops 4718592 | bytes 393472 | tf_op jit(solution)/shard_map/pi,lxaiz->lxapz/dot_general | solution.py:110
  8.0 0.6 copy.70
  8.6 0.7 copy.57
  9.3 0.7 copy.61
  10.1 0.5 fusion.76
  10.6 0.5 fusion.49
  11.2 0.7 convolution_bitcast_fusion.2
  11.9 0.7 convolution_bitcast_fusion.1
  12.6 0.8 reshape.439
  13.5 0.5 mul.717
  14.0 0.8 fusion.94
  14.9 1.0 slice_bitcast_fusion
  16.1 1.1 reshape.470
  17.2 0.5 reshape.467
  17.7 0.7 multiply_multiply_fusion.1
  18.5 1.0 add_multiply_fusion.1
  19.8 0.7 copy.69
  20.8 1.1 reshape.478
  21.9 0.5 reshape.475
  22.8 3.1 %broadcast_multiply_fusion.6 = (f32[3,12,24,192]{3,2,1,0:T(8,128)S(1)}, f32[3,12,24,192]{3,2,1,0:T(8,128)S(1)}, f32[3,12,24,192]{3,2,1,0:T(8,128)}) fusion(f32[12,24,192]{2,1,0:T(8,128)} %get-tuple-element.11, f32[12,24,192]{2,1,0:T(8,128)} %get-tuple-element.12, f32[12,24,192]{2,1,0:T(8,128)} %get-tuple-element.13, ...), kind=kOutput, calls=%fused_computation.42 | convolution fusion | flops 255467520 | bytes 3416064 | tf_op jit(solution)/shard_map/lxyzk,kq->lxyzq/dot_general | solution.py:121
  26.0 2.0 %fusion.82 = f32[3,12,2,12,128]{4,3,2,1,0:T(8,128)S(1)} fusion(f32[3,12,2,12,192]{4,3,2,1,0:T(8,128)S(1)} %dot_general.184, f32[192,128,1,1,1]{0,1,2,3,4:T(8,128)} %reshape.478), kind=kOutput, calls=%fused_computation.147 | convolution fusion | flops 254803968 | bytes 1204224 | tf_op jit(solution)/shard_map/lxyzk,kq->lxyzq/dot_general | solution.py:121
  28.0 1.2 convolution_bitcast_fusion.6
  29.2 1.3 %dot_general.174 = f32[3,12,2,12,192]{4,3,2,1,0:T(8,128)S(1)} reshape(f32[3,12,24,192]{3,2,1,0:T(8,128)} %get-tuple-element.10) | data formatting | bytes 1327104 | tf_op jit(solution)/shard_map/lxyzk,kq->lxyzq/dot_general | solution.py:121
  30.5 1.1 fusion.88
  31.6 1.3 %fusion.90 = f32[3,12,2,12,128]{4,3,2,1,0:T(8,128)S(1)} fusion(f32[3,12,2,12,192]{4,3,2,1,0:T(8,128)S(1)} %dot_general.174, f32[192,128,1,1,1]{0,1,2,3,4:T(8,128)S(1)} %reshape.475), kind=kOutput, calls=%fused_computation.155 | convolution fusion | flops 254803968 | bytes 1204224 | tf_op jit(solution)/shard_map/lxyzk,kq->lxyzq/dot_general | solution.py:121
  35.0 0.5 fusion.5
  35.5 0.5 fusion.4
  35.9 0.5 fusion.3
  36.5 11.7 %collective-permute-start = (f32[4,1,16,128]{3,1,2,0:T(1,128)S(1)}, f32[4,1,16,128]{3,1,2,0:T(1,128)S(1)}, u32[]{:S(2)}, u32[]{:S(2)}) collective-permute-start(f32[4,1,16,128]{3,1,2,0:T(1,128)S(1)} %get-tuple-element.20), channel_id=1, source_target_pairs={{8,0},{16,8},{24,16},{32,24},{40,32},{48,40},{56,48},{64,56},{72,6... | collective-permute-start | bytes 98312 | tf_op jit(solution)/shard_map/ppermute | solution.py:58
  48.2 1.9 %collective-permute-start.1 = (f32[4,1,16,128]{3,1,2,0:T(1,128)S(1)}, f32[4,1,16,128]{3,1,2,0:T(1,128)S(1)}, u32[]{:S(2)}, u32[]{:S(2)}) collective-permute-start(f32[4,1,16,128]{3,1,2,0:T(1,128)S(1)} %get-tuple-element.21), channel_id=1, source_target_pairs={{0,8},{8,16},{16,24},{24,32},{32,40},{40,48},{48,56},{56,64},{64,7... | collective-permute-start | bytes 98312 | tf_op jit(solution)/shard_map/ppermute | solution.py:55
  50.3 8.6 %collective-permute-done.1 = f32[4,1,16,128]{3,1,2,0:T(1,128)S(1)} collective-permute-done((f32[4,1,16,128]{3,1,2,0:T(1,128)S(1)}, f32[4,1,16,128]{3,1,2,0:T(1,128)S(1)}, u32[]{:S(2)}, u32[]{:S(2)}) %collective-permute-start.1) | collective-permute-done | bytes 32800 | tf_op jit(solution)/shard_map/ppermute | solution.py:55
  59.2 4.0 %collective-permute-start.2 = (f32[4,8,16,1]{3,1,2,0:T(8,128)S(1)}, f32[4,8,16,1]{3,1,2,0:T(8,128)S(1)}, u32[]{:S(2)}, u32[]{:S(2)}) collective-permute-start(f32[4,8,16,1]{3,1,2,0:T(8,128)S(1)} %get-tuple-element.18), channel_id=1, source_target_pairs={{1,0},{2,1},{3,2},{4,3},{5,4},{6,5},{7,6},{9,8},{10,9},{11,10},{12... | collective-permute-start | bytes 6152 | tf_op jit(solution)/shard_map/ppermute | solution.py:58
  63.2 8.9 %collective-permute-start.3 = (f32[4,8,16,1]{3,1,2,0:T(8,128)S(1)}, f32[4,8,16,1]{3,1,2,0:T(8,128)S(1)}, u32[]{:S(2)}, u32[]{:S(2)}) collective-permute-start(f32[4,8,16,1]{3,1,2,0:T(8,128)S(1)} %get-tuple-element.19), channel_id=1, source_target_pairs={{0,1},{1,2},{2,3},{3,4},{4,5},{5,6},{6,7},{8,9},{9,10},{10,11},{11... | collective-permute-start | bytes 6152 | tf_op jit(solution)/shard_map/ppermute | solution.py:55
  72.1 2.1 %collective-permute-done.2 = f32[4,8,16,1]{3,1,2,0:T(8,128)S(1)} collective-permute-done((f32[4,8,16,1]{3,1,2,0:T(8,128)S(1)}, f32[4,8,16,1]{3,1,2,0:T(8,128)S(1)}, u32[]{:S(2)}, u32[]{:S(2)}) %collective-permute-start.2) | collective-permute-done | bytes 2080 | tf_op jit(solution)/shard_map/ppermute | solution.py:58
  74.2 1.2 collective-permute-done.3
  75.8 0.6 multiply_bitcast_fusion.1
  76.8 0.5 fusion.126
  78.9 1.0 convolution_add_fusion
  79.9 0.7 convolution_bitcast_fusion
  80.6 0.8 reshape.452
  81.4 2.8 %broadcast_multiply_fusion.5 = (f32[3,12,24,192]{3,2,1,0:T(8,128)}, f32[3,12,24,192]{3,2,1,0:T(8,128)S(1)}, f32[3,12,24,192]{3,2,1,0:T(8,128)S(1)}) fusion(f32[12,24,192]{2,1,0:T(8,128)S(1)} %copy-done.6, f32[12,24,192]{2,1,0:T(8,128)S(1)} %copy-done.7, f32[12,24,192]{2,1,0:T(8,128)S(1)} %copy-done.8, f32[12,24,192]{2,1,0:T(8,128)S(1)} %copy-done.10, ...), kind=kOutput, calls=%fused_computation.41 | convolution fusion | flops 255467520 | bytes 3416064 | tf_op jit(solution)/shard_map/lxyzk,kq->lxyzq/dot_general | solution.py:121
  84.3 1.3 %dot_general.211 = f32[3,12,2,12,192]{4,3,2,1,0:T(8,128)S(1)} reshape(f32[3,12,24,192]{3,2,1,0:T(8,128)} %get-tuple-element.5) | data formatting | bytes 1327104 | tf_op jit(solution)/shard_map/lxyzk,kq->lxyzq/dot_general | solution.py:121
  85.5 2.0 %fusion.80 = f32[3,12,2,12,128]{4,3,2,1,0:T(8,128)S(1)} fusion(f32[3,12,2,12,192]{4,3,2,1,0:T(8,128)S(1)} %dot_general.211, f32[192,128,1,1,1]{0,1,2,3,4:T(8,128)} %reshape.478), kind=kOutput, calls=%fused_computation.145 | convolution fusion | flops 254803968 | bytes 1204224 | tf_op jit(solution)/shard_map/lxyzk,kq->lxyzq/dot_general | solution.py:121
  87.5 1.2 convolution_bitcast_fusion.3
  88.8 1.1 fusion.84
  90.5 1.1 fusion.86
  92.1 0.5 fusion.2
  92.6 0.5 fusion.1
  93.1 0.5 fusion
  93.6 7.1 %collective-permute-start.4 = (f32[3,1,16,128]{3,1,2,0:T(1,128)S(1)}, f32[3,1,16,128]{3,1,2,0:T(1,128)S(1)}, u32[]{:S(2)}, u32[]{:S(2)}) collective-permute-start(f32[3,1,16,128]{3,1,2,0:T(1,128)S(1)} %get-tuple-element.26), channel_id=1, source_target_pairs={{8,0},{16,8},{24,16},{32,24},{40,32},{48,40},{56,48},{64,56},{72,6... | collective-permute-start | bytes 73736 | tf_op jit(solution)/shard_map/ppermute | solution.py:58
  100.7 1.9 %collective-permute-start.5 = (f32[3,1,16,128]{3,1,2,0:T(1,128)S(1)}, f32[3,1,16,128]{3,1,2,0:T(1,128)S(1)}, u32[]{:S(2)}, u32[]{:S(2)}) collective-permute-start(f32[3,1,16,128]{3,1,2,0:T(1,128)S(1)} %get-tuple-element.27), channel_id=1, source_target_pairs={{0,8},{8,16},{16,24},{24,32},{32,40},{40,48},{48,56},{56,64},{64,7... | collective-permute-start | bytes 73736 | tf_op jit(solution)/shard_map/ppermute | solution.py:55
  102.6 8.9 %collective-permute-done.5 = f32[3,1,16,128]{3,1,2,0:T(1,128)S(1)} collective-permute-done((f32[3,1,16,128]{3,1,2,0:T(1,128)S(1)}, f32[3,1,16,128]{3,1,2,0:T(1,128)S(1)}, u32[]{:S(2)}, u32[]{:S(2)}) %collective-permute-start.5) | collective-permute-done | bytes 24608 | tf_op jit(solution)/shard_map/ppermute | solution.py:55
  111.8 1.9 %collective-permute-start.6 = (f32[3,8,16,1]{3,1,2,0:T(8,128)S(1)}, f32[3,8,16,1]{3,1,2,0:T(8,128)S(1)}, u32[]{:S(2)}, u32[]{:S(2)}) collective-permute-start(f32[3,8,16,1]{3,1,2,0:T(8,128)S(1)} %get-tuple-element.24), channel_id=1, source_target_pairs={{1,0},{2,1},{3,2},{4,3},{5,4},{6,5},{7,6},{9,8},{10,9},{11,10},{12... | collective-permute-start | bytes 4616 | tf_op jit(solution)/shard_map/ppermute | solution.py:58
  113.7 7.5 %collective-permute-start.7 = (f32[3,8,16,1]{3,1,2,0:T(8,128)S(1)}, f32[3,8,16,1]{3,1,2,0:T(8,128)S(1)}, u32[]{:S(2)}, u32[]{:S(2)}) collective-permute-start(f32[3,8,16,1]{3,1,2,0:T(8,128)S(1)} %get-tuple-element.25), channel_id=1, source_target_pairs={{0,1},{1,2},{2,3},{3,4},{4,5},{5,6},{6,7},{8,9},{9,10},{10,11},{11... | collective-permute-start | bytes 4616 | tf_op jit(solution)/shard_map/ppermute | solution.py:55
  121.3 1.4 %collective-permute-done.6 = f32[3,8,16,1]{3,1,2,0:T(8,128)S(1)} collective-permute-done((f32[3,8,16,1]{3,1,2,0:T(8,128)S(1)}, f32[3,8,16,1]{3,1,2,0:T(8,128)S(1)}, u32[]{:S(2)}, u32[]{:S(2)}) %collective-permute-start.6) | collective-permute-done | bytes 1568 | tf_op jit(solution)/shard_map/ppermute | solution.py:58
  122.7 1.2 collective-permute-done.7
  124.3 0.7 copy.103
  (178 shorter events, 8.5 us)
Async XLA Ops:
  0.0 10.6 %copy-start = (f32[3,8,16,128]{3,2,1,0:T(8,128)S(1)}, f32[3,8,16,128]{3,2,1,0:T(8,128)}, u32[]{:S(2)}) copy-start(f32[3,8,16,128]{3,2,1,0:T(8,128)} %param.11) | copy-start | bytes 589828
  0.0 7.9 %copy-start.34 = (bf16[3,8,16,128]{3,2,1,0:T(8,128)(2,1)S(1)}, bf16[3,8,16,128]{3,2,1,0:T(8,128)(2,1)}, u32[]{:S(2)}) copy-start(bf16[3,8,16,128]{3,2,1,0:T(8,128)(2,1)} %param.12) | copy-start | bytes 294916
  0.0 9.3 %copy-start.35 = (bf16[3,8,16,128]{3,2,1,0:T(8,128)(2,1)S(1)}, bf16[3,8,16,128]{3,2,1,0:T(8,128)(2,1)}, u32[]{:S(2)}) copy-start(bf16[3,8,16,128]{3,2,1,0:T(8,128)(2,1)} %param.13) | copy-start | bytes 294916
  6.4 12.0 %copy-start.2 = (f32[3,8,16,128]{3,1,2,0:T(8,128)}, f32[3,8,16,128]{3,1,2,0:T(8,128)S(1)}, u32[]{:S(2)}) copy-start(f32[3,8,16,128]{3,1,2,0:T(8,128)S(1)} %convolution_bitcast_fusion.23) | copy-start | bytes 589828
  6.5 3.6 %copy-start.1 = (f32[3,8,16,128]{3,2,1,0:T(8,128)S(1)}, f32[3,8,16,128]{3,2,1,0:T(8,128)}, u32[]{:S(2)}) copy-start(f32[3,8,16,128]{3,2,1,0:T(8,128)} %param.10) | copy-start | bytes 589828
  6.5 3.6 %copy-start.32 = (f32[12,8,1,1]{0,1,3,2:T(8,128)S(1)}, f32[12,8,1,1]{0,1,3,2:T(8,128)}, u32[]{:S(2)}) copy-start(f32[12,8,1,1]{0,1,3,2:T(8,128)} %constant.92) | copy-start | bytes 1156
  7.9 10.5 %copy-start.4 = (f32[3,8,2,8,128]{4,1,3,2,0:T(8,128)}, f32[3,8,2,8,128]{4,1,3,2,0:T(8,128)S(1)}, u32[]{:S(2)}) copy-start(f32[3,8,2,8,128]{4,1,3,2,0:T(8,128)S(1)} %copy.60) | copy-start | bytes 589828
  8.0 3.2 %copy-start.33 = (f32[12,8,1,1,1]{0,1,4,3,2:T(8,128)S(1)}, f32[12,8,1,1,1]{0,1,4,3,2:T(8,128)}, u32[]{:S(2)}) copy-start(f32[12,8,1,1,1]{0,1,4,3,2:T(8,128)} %constant.93) | copy-start | bytes 1156
  9.3 9.1 %copy-start.29 = (f32[8,16,128]{2,0,1:T(8,128)}, f32[8,16,128]{2,0,1:T(8,128)S(1)}, u32[]{:S(2)}) copy-start(f32[8,16,128]{2,0,1:T(8,128)S(1)} %copy.65) | copy-start | bytes 196612
  10.0 8.4 %copy-start.17 = (f32[8,16,128]{2,0,1:T(8,128)}, f32[8,16,128]{2,0,1:T(8,128)S(1)}, u32[]{:S(2)}) copy-start(f32[8,16,128]{2,0,1:T(8,128)S(1)} %copy.59) | copy-start | bytes 196612
  10.1 8.4 %copy-start.15 = (f32[8,16,128]{2,0,1:T(8,128)}, f32[8,16,128]{2,0,1:T(8,128)S(1)}, u32[]{:S(2)}) copy-start(f32[8,16,128]{2,0,1:T(8,128)S(1)} %copy.66) | copy-start | bytes 196612
  11.9 1.5 %copy-start.47 = (f32[8,12]{1,0:T(8,128)S(1)}, f32[8,12]{1,0:T(8,128)}, u32[]{:S(2)}) copy-start(f32[8,12]{1,0:T(8,128)} %constant.89) | copy-start | bytes 1156
  16.1 1.6 %copy-start.38 = (f32[8,16,128]{2,1,0:T(8,128)S(1)}, f32[8,16,128]{2,1,0:T(8,128)}, u32[]{:S(2)}) copy-start(f32[8,16,128]{2,1,0:T(8,128)} %param.14) | copy-start | bytes 196612
  17.2 2.3 %copy-start.37 = (f32[8,8,1,1,1]{1,0,4,3,2:T(8,128)S(1)}, f32[8,8,1,1,1]{1,0,4,3,2:T(8,128)}, u32[]{:S(2)}) copy-start(f32[8,8,1,1,1]{1,0,4,3,2:T(8,128)} %constant.91) | copy-start | bytes 772
  17.7 1.8 %copy-start.24 = (f32[128,128,1,1]{1,0,2,3:T(8,128)}, f32[128,128,1,1]{1,0,2,3:T(8,128)S(1)}, u32[]{:S(2)}) copy-start(f32[128,128,1,1]{1,0,2,3:T(8,128)S(1)} %reshape.467) | copy-start | bytes 196612
  17.7 2.9 %copy-start.43 = (f32[12,8]{0,1:T(8,128)S(1)}, f32[12,8]{0,1:T(8,128)}, u32[]{:S(2)}) copy-start(f32[12,8]{0,1:T(8,128)} %constant.81.clone) | copy-start | bytes 1156
  17.7 2.9 %copy-start.44 = (f32[12,8]{0,1:T(8,128)S(1)}, f32[12,8]{0,1:T(8,128)}, u32[]{:S(2)}) copy-start(f32[12,8]{0,1:T(8,128)} %constant.80.clone) | copy-start | bytes 1156
  20.8 1.6 %copy-start.39 = (f32[12,24]{1,0:T(8,128)S(1)}, f32[12,24]{1,0:T(8,128)}, u32[]{:S(2)}) copy-start(f32[12,24]{1,0:T(8,128)} %broadcast_multiply_fusion.12) | copy-start | bytes 3460
  22.5 3.3 %copy-start.9 = (f32[12,24,192]{2,1,0:T(8,128)}, f32[12,24,192]{2,1,0:T(8,128)S(1)}, u32[]{:S(2)}) copy-start(f32[12,24,192]{2,1,0:T(8,128)S(1)} %broadcast_multiply_fusion.11) | copy-start | bytes 663556
  31.6 1.9 %copy-start.41 = (f32[12,8,1,1,1]{0,1,4,3,2:T(8,128)S(1)}, f32[12,8,1,1,1]{0,1,4,3,2:T(8,128)}, u32[]{:S(2)}) copy-start(f32[12,8,1,1,1]{0,1,4,3,2:T(8,128)} %constant.95) | copy-start | bytes 1156
  32.9 1.1 copy-start.3
  32.9 1.1 copy-start.13
  32.9 1.1 copy-start.14
  33.0 1.1 copy-start.18
  33.0 1.2 copy-start.21
  33.0 1.2 copy-start.28
  33.0 1.2 copy-start.36
  33.5 1.1 copy-start.16
  33.5 1.1 copy-start.23
  33.5 1.1 copy-start.27
  34.6 1.3 %copy-start.19 = (f32[3,12,16,128]{3,2,1,0:T(8,128)S(1)}, f32[3,12,16,128]{3,2,1,0:T(8,128)}, u32[]{:S(2)}) copy-start(f32[3,12,16,128]{3,2,1,0:T(8,128)} %convolution_bitcast_fusion.6) | copy-start | bytes 884740
  35.0 1.4 %copy-start.26 = (f32[1,8,16,128]{3,1,2,0:T(8,128)S(1)}, f32[1,8,16,128]{3,1,2,0:T(8,128)}, u32[]{:S(2)}) copy-start(f32[1,8,16,128]{3,1,2,0:T(8,128)} %get-tuple-element.35) | copy-start | bytes 196612
  36.5 13.8 %collective-permute-start = (f32[4,1,16,128]{3,1,2,0:T(1,128)S(1)}, f32[4,1,16,128]{3,1,2,0:T(1,128)S(1)}, u32[]{:S(2)}, u32[]{:S(2)}) collective-permute-start(f32[4,1,16,128]{3,1,2,0:T(1,128)S(1)} %get-tuple-element.20), channel_id=1, source_target_pairs={{8,0},{16,8},{24,16},{32,24},{40,32},{48,40},{56,48},{64,56},{72,6... | collective-permute-start | bytes 98312 | tf_op jit(solution)/shard_map/ppermute | solution.py:58
  48.2 10.7 %collective-permute-start.1 = (f32[4,1,16,128]{3,1,2,0:T(1,128)S(1)}, f32[4,1,16,128]{3,1,2,0:T(1,128)S(1)}, u32[]{:S(2)}, u32[]{:S(2)}) collective-permute-start(f32[4,1,16,128]{3,1,2,0:T(1,128)S(1)} %get-tuple-element.21), channel_id=1, source_target_pairs={{0,8},{8,16},{16,24},{24,32},{32,40},{40,48},{48,56},{56,64},{64,7... | collective-permute-start | bytes 98312 | tf_op jit(solution)/shard_map/ppermute | solution.py:55
  50.2 8.7 %copy-start.52 = (pred[8]{0:T(512)(128)(4,1)}, pred[8]{0:T(512)(128)(4,1)S(1)}, u32[]{:S(2)}) copy-start(pred[8]{0:T(512)(128)(4,1)S(1)} %get-tuple-element.44) | copy-start | bytes 28
  50.2 8.7 %copy-start.54 = (pred[8]{0:T(512)(128)(4,1)}, pred[8]{0:T(512)(128)(4,1)S(1)}, u32[]{:S(2)}) copy-start(pred[8]{0:T(512)(128)(4,1)S(1)} %get-tuple-element.45) | copy-start | bytes 28
  50.2 25.4 %copy-start.48 = (pred[128]{0:T(512)(128)(4,1)}, pred[128]{0:T(512)(128)(4,1)S(1)}, u32[]{:S(2)}) copy-start(pred[128]{0:T(512)(128)(4,1)S(1)} %get-tuple-element.46) | copy-start | bytes 388
  50.2 25.4 %copy-start.50 = (pred[128]{0:T(512)(128)(4,1)}, pred[128]{0:T(512)(128)(4,1)S(1)}, u32[]{:S(2)}) copy-start(pred[128]{0:T(512)(128)(4,1)S(1)} %get-tuple-element.47) | copy-start | bytes 388
  50.2 25.4 %copy-start.56 = (pred[16]{0:T(512)(128)(4,1)}, pred[16]{0:T(512)(128)(4,1)S(1)}, u32[]{:S(2)}) copy-start(pred[16]{0:T(512)(128)(4,1)S(1)} %get-tuple-element.48) | copy-start | bytes 52
  50.2 25.4 %copy-start.58 = (pred[16]{0:T(512)(128)(4,1)}, pred[16]{0:T(512)(128)(4,1)S(1)}, u32[]{:S(2)}) copy-start(pred[16]{0:T(512)(128)(4,1)S(1)} %get-tuple-element.49) | copy-start | bytes 52
  59.2 15.0 %collective-permute-start.2 = (f32[4,8,16,1]{3,1,2,0:T(8,128)S(1)}, f32[4,8,16,1]{3,1,2,0:T(8,128)S(1)}, u32[]{:S(2)}, u32[]{:S(2)}) collective-permute-start(f32[4,8,16,1]{3,1,2,0:T(8,128)S(1)} %get-tuple-element.18), channel_id=1, source_target_pairs={{1,0},{2,1},{3,2},{4,3},{5,4},{6,5},{7,6},{9,8},{10,9},{11,10},{12... | collective-permute-start | bytes 6152 | tf_op jit(solution)/shard_map/ppermute | solution.py:58
  63.2 12.2 %collective-permute-start.3 = (f32[4,8,16,1]{3,1,2,0:T(8,128)S(1)}, f32[4,8,16,1]{3,1,2,0:T(8,128)S(1)}, u32[]{:S(2)}, u32[]{:S(2)}) collective-permute-start(f32[4,8,16,1]{3,1,2,0:T(8,128)S(1)} %get-tuple-element.19), channel_id=1, source_target_pairs={{0,1},{1,2},{2,3},{3,4},{4,5},{5,6},{6,7},{8,9},{9,10},{10,11},{11... | collective-permute-start | bytes 6152 | tf_op jit(solution)/shard_map/ppermute | solution.py:55
  72.1 4.5 %copy-start.60 = (f32[128]{0:T(128)}, f32[128]{0:T(128)S(1)}, u32[]{:S(2)}) copy-start(f32[128]{0:T(128)S(1)} %and_convert_fusion) | copy-start | bytes 1540
  76.4 1.3 %copy-start.25 = (f32[128,128,1,1]{1,0,2,3:T(8,128)S(1)}, f32[128,128,1,1]{1,0,2,3:T(8,128)}, u32[]{:S(2)}) copy-start(f32[128,128,1,1]{1,0,2,3:T(8,128)} %copy-done.24) | copy-start | bytes 196612
  76.4 1.3 %copy-start.30 = (f32[8,16,128]{2,0,1:T(8,128)S(1)}, f32[8,16,128]{2,0,1:T(8,128)}, u32[]{:S(2)}) copy-start(f32[8,16,128]{2,0,1:T(8,128)} %copy-done.29) | copy-start | bytes 196612
  79.9 1.5 %copy-start.6 = (f32[12,24,192]{2,1,0:T(8,128)S(1)}, f32[12,24,192]{2,1,0:T(8,128)}, u32[]{:S(2)}) copy-start(f32[12,24,192]{2,1,0:T(8,128)} %get-tuple-element.11) | copy-start | bytes 663556
  79.9 1.5 %copy-start.7 = (f32[12,24,192]{2,1,0:T(8,128)S(1)}, f32[12,24,192]{2,1,0:T(8,128)}, u32[]{:S(2)}) copy-start(f32[12,24,192]{2,1,0:T(8,128)} %get-tuple-element.12) | copy-start | bytes 663556
  79.9 1.5 %copy-start.8 = (f32[12,24,192]{2,1,0:T(8,128)S(1)}, f32[12,24,192]{2,1,0:T(8,128)}, u32[]{:S(2)}) copy-start(f32[12,24,192]{2,1,0:T(8,128)} %get-tuple-element.13) | copy-start | bytes 663556
  79.9 1.5 %copy-start.10 = (f32[12,24,192]{2,1,0:T(8,128)S(1)}, f32[12,24,192]{2,1,0:T(8,128)}, u32[]{:S(2)}) copy-start(f32[12,24,192]{2,1,0:T(8,128)} %copy-done.9) | copy-start | bytes 663556
  88.8 1.1 copy-start.42
  90.5 1.6 %copy-start.22 = (f32[3,8,16,128]{3,1,2,0:T(8,128)S(1)}, f32[3,8,16,128]{3,1,2,0:T(8,128)}, u32[]{:S(2)}) copy-start(f32[3,8,16,128]{3,1,2,0:T(8,128)} %convolution_add_fusion) | copy-start | bytes 589828
  91.6 1.4 %copy-start.20 = (f32[3,12,16,128]{3,2,1,0:T(8,128)S(1)}, f32[3,12,16,128]{3,2,1,0:T(8,128)}, u32[]{:S(2)}) copy-start(f32[3,12,16,128]{3,2,1,0:T(8,128)} %convolution_bitcast_fusion.3) | copy-start | bytes 884740
  92.1 19.5 %copy-start.53 = (pred[8]{0:T(512)(128)(4,1)S(1)}, pred[8]{0:T(512)(128)(4,1)}, u32[]{:S(2)}) copy-start(pred[8]{0:T(512)(128)(4,1)} %copy-done.52) | copy-start | bytes 28
  92.1 19.5 %copy-start.55 = (pred[8]{0:T(512)(128)(4,1)S(1)}, pred[8]{0:T(512)(128)(4,1)}, u32[]{:S(2)}) copy-start(pred[8]{0:T(512)(128)(4,1)} %copy-done.54) | copy-start | bytes 28
  93.0 30.9 %copy-start.49 = (pred[128]{0:T(512)(128)(4,1)S(1)}, pred[128]{0:T(512)(128)(4,1)}, u32[]{:S(2)}) copy-start(pred[128]{0:T(512)(128)(4,1)} %copy-done.48) | copy-start | bytes 388
  93.0 30.8 %copy-start.51 = (pred[128]{0:T(512)(128)(4,1)S(1)}, pred[128]{0:T(512)(128)(4,1)}, u32[]{:S(2)}) copy-start(pred[128]{0:T(512)(128)(4,1)} %copy-done.50) | copy-start | bytes 388
  93.5 30.6 %copy-start.31 = (f32[8,16,128]{2,0,1:T(8,128)S(1)}, f32[8,16,128]{2,0,1:T(8,128)}, u32[]{:S(2)}) copy-start(f32[8,16,128]{2,0,1:T(8,128)} %get-tuple-element.14) | copy-start | bytes 196612
  93.5 30.6 %copy-start.57 = (pred[16]{0:T(512)(128)(4,1)S(1)}, pred[16]{0:T(512)(128)(4,1)}, u32[]{:S(2)}) copy-start(pred[16]{0:T(512)(128)(4,1)} %copy-done.56) | copy-start | bytes 52
  93.5 30.6 %copy-start.59 = (pred[16]{0:T(512)(128)(4,1)S(1)}, pred[16]{0:T(512)(128)(4,1)}, u32[]{:S(2)}) copy-start(pred[16]{0:T(512)(128)(4,1)} %copy-done.58) | copy-start | bytes 52
  93.6 30.6 %copy-start.61 = (f32[128]{0:T(128)S(1)}, f32[128]{0:T(128)}, u32[]{:S(2)}) copy-start(f32[128]{0:T(128)} %copy-done.60) | copy-start | bytes 1540
  93.6 9.0 %collective-permute-start.4 = (f32[3,1,16,128]{3,1,2,0:T(1,128)S(1)}, f32[3,1,16,128]{3,1,2,0:T(1,128)S(1)}, u32[]{:S(2)}, u32[]{:S(2)}) collective-permute-start(f32[3,1,16,128]{3,1,2,0:T(1,128)S(1)} %get-tuple-element.26), channel_id=1, source_target_pairs={{8,0},{16,8},{24,16},{32,24},{40,32},{48,40},{56,48},{64,56},{72,6... | collective-permute-start | bytes 73736 | tf_op jit(solution)/shard_map/ppermute | solution.py:58
  100.7 10.9 %collective-permute-start.5 = (f32[3,1,16,128]{3,1,2,0:T(1,128)S(1)}, f32[3,1,16,128]{3,1,2,0:T(1,128)S(1)}, u32[]{:S(2)}, u32[]{:S(2)}) collective-permute-start(f32[3,1,16,128]{3,1,2,0:T(1,128)S(1)} %get-tuple-element.27), channel_id=1, source_target_pairs={{0,8},{8,16},{16,24},{24,32},{32,40},{40,48},{48,56},{56,64},{64,7... | collective-permute-start | bytes 73736 | tf_op jit(solution)/shard_map/ppermute | solution.py:55
  111.8 10.9 %collective-permute-start.6 = (f32[3,8,16,1]{3,1,2,0:T(8,128)S(1)}, f32[3,8,16,1]{3,1,2,0:T(8,128)S(1)}, u32[]{:S(2)}, u32[]{:S(2)}) collective-permute-start(f32[3,8,16,1]{3,1,2,0:T(8,128)S(1)} %get-tuple-element.24), channel_id=1, source_target_pairs={{1,0},{2,1},{3,2},{4,3},{5,4},{6,5},{7,6},{9,8},{10,9},{11,10},{12... | collective-permute-start | bytes 4616 | tf_op jit(solution)/shard_map/ppermute | solution.py:58
  113.7 10.2 %collective-permute-start.7 = (f32[3,8,16,1]{3,1,2,0:T(8,128)S(1)}, f32[3,8,16,1]{3,1,2,0:T(8,128)S(1)}, u32[]{:S(2)}, u32[]{:S(2)}) collective-permute-start(f32[3,8,16,1]{3,1,2,0:T(8,128)S(1)} %get-tuple-element.25), channel_id=1, source_target_pairs={{0,1},{1,2},{2,3},{3,4},{4,5},{5,6},{6,7},{8,9},{9,10},{10,11},{11... | collective-permute-start | bytes 4616 | tf_op jit(solution)/shard_map/ppermute | solution.py:55
  (6 other events, 5.6 us)
where the time goes:
time: 126 us; the launch traced here: 125 us
  starting transfers between devices  45 us (36%)
  matrix products  33.1 us (26%)
  waiting for transfers between devices  23.4 us (19%)
  local copies, waits for them, and re-layouts  17 us (13%)
  other arithmetic  5.19 us (4%)
  between operations  1.26 us (1%)
    ppermute x4, starting transfers between devices, padded_2(): lax.ppermute(lax.slice_in_dim(block, 0, width, axis=dim), axis, backward)  24.7 us
    ppermute x4, starting transfers between devices, padded_2(): lax.ppermute(lax.slice_in_dim(block, block.shape[dim] - width, None, axis...  20.3 us
    ppermute x4, waiting for transfers between devices, padded_2(): lax.ppermute(lax.slice_in_dim(block, block.shape[dim] - width, None, axis...  19.9 us
    dot_general x13, matrix products, along_third(): result = jnp.einsum('lxyzk,kq->lxyzq', blocks, kron_table, precision=HIGH)  17.9 us
    dot_general x13, matrix products, along_second(): result = jnp.einsum('pi,lxaiz->lxapz', matrix, blocks, precision=HIGH)  8.56 us
    dot_general x13, matrix products, along_first(): result = jnp.einsum('pi,laimz->lapmz', matrix, blocks, precision=HIGH)  6.66 us
    mul x5, local copies, waits for them, and re-layouts, along_third(): kron_table = jnp.kron(jnp.eye(group_size, dtype=jnp.float32), matrix.T)  3.68 us
    ppermute x4, waiting for transfers between devices, padded_2(): lax.ppermute(lax.slice_in_dim(block, 0, width, axis=dim), axis, backward)  3.5 us
  transfers between devices with their start and end apart: 8, of which 6 were waited for; matrix products, arithmetic and copies ran while one was open for 0% of the time, Pallas kernels for 0%

commit v1 on v0

v1 whole, which is shorter than its diff:
```python
import functools

import jax
import jax.numpy as jnp
import ml_dtypes
import numpy as np
from jax import lax
from jax.experimental import pallas as pl
from jax.experimental.pallas import tpu as pltpu
from jax.sharding import PartitionSpec as P

VISCOSITY = 0.05
STEP_SIZE = 0.01
GLL_INNER = [
    -0.8717401485096066,
    -0.5917001814331423,
    -0.2092992179024789,
    0.2092992179024789,
    0.5917001814331423,
    0.8717401485096066,
]
GAUSS_POINTS = [
    -0.9815606342467192,
    -0.9041172563704749,
    -0.7699026741943047,
    -0.5873179542866175,
    -0.3678314989981802,
    -0.1252334085114689,
    0.1252334085114689,
    0.3678314989981802,
    0.5873179542866175,
    0.7699026741943047,
    0.9041172563704749,
    0.9815606342467192,
]
GAUSS_WEIGHTS = [
    0.0471753363865118,
    0.1069393259953184,
    0.1600783285433462,
    0.2031674267230659,
    0.2334925365383548,
    0.2491470458134028,
    0.2491470458134028,
    0.2334925365383548,
    0.2031674267230659,
    0.1600783285433462,
    0.1069393259953184,
    0.0471753363865118,
]
MESH = pl.DeviceIdType.MESH
F32 = jnp.float32
BF16 = jnp.bfloat16


def legendre_seven(points):
    previous = points * 0.0 + 1.0
    current = points
    for degree in range(1, 7):
        following = ((2.0 * degree + 1.0) * points * current - degree * previous) / (degree + 1.0)
        previous = current
        current = following
    return current


def node_tables():
    gll_nodes = np.array([-1.0] + GLL_INNER + [1.0])
    values = legendre_seven(gll_nodes)
    node_weights = 2.0 / (56.0 * values * values)
    identity = np.eye(8, dtype=bool)
    spacing = gll_nodes[:, None] - gll_nodes[None, :]
    derivative = np.where(
        identity, 0.0, values[:, None] / (values[None, :] * np.where(identity, 1.0, spacing))
    )
    corner_terms = np.concatenate([np.array([-14.0]), np.zeros(6), np.array([14.0])])
    derivative = derivative + np.eye(8) * corner_terms[None, :]
    gauss_nodes = np.array(GAUSS_POINTS)
    gauss_weights = np.array(GAUSS_WEIGHTS)
    numerators = gauss_nodes[:, None, None] - gll_nodes[None, None, :]
    denominators = np.where(identity, 1.0, spacing)[None]
    ratios = np.where(identity[None], 1.0, numerators / denominators)
    interpolation = ratios.prod(axis=2)
    slope_interp = interpolation @ derivative
    return tuple(
        np.asarray(member, np.float32).astype(np.float64)
        for member in (derivative, node_weights, interpolation, slope_interp, gauss_weights)
    )


def halves(matrix):
    high = matrix.astype(np.float32).astype(ml_dtypes.bfloat16)
    low = (matrix - high.astype(np.float64)).astype(np.float32).astype(ml_dtypes.bfloat16)
    return high, low


def left_table(matrix):
    high, low = halves(matrix)
    return np.concatenate([high, high, low], axis=1)


def right_table(matrix):
    high, low = halves(matrix)
    return np.concatenate([high, high, low], axis=0)


def pad_to(matrix, rows, columns):
    return np.pad(matrix, ((0, rows - matrix.shape[0]), (0, columns - matrix.shape[1])))


def operator_tables():
    dm, rho, jm, dj, sigma = node_tables()
    eye8, eye16 = np.eye(8), np.eye(16)
    forward_z = np.concatenate(
        [np.kron(eye16, dm.T), pad_to(np.kron(eye16, jm.T), 128, 256)], axis=1
    )
    back_z = np.concatenate(
        [
            pad_to(np.kron(eye16, jm), 256, 128),
            pad_to(np.kron(eye16, dj), 256, 128),
            np.kron(eye16, dm),
        ],
        axis=0,
    )
    grad_xy = np.concatenate([np.kron(dm, eye8), np.kron(eye8, dm)], axis=0)
    interp_xy = np.kron(jm, jm)
    back_12 = np.concatenate([np.kron(dj.T, jm.T), np.kron(jm.T, dj.T)], axis=1)
    back_3 = np.kron(jm.T, jm.T)
    back_grad = np.concatenate([np.kron(dm.T, eye8), np.kron(eye8, dm.T)], axis=1)
    fine_z = pad_to(np.tile(sigma, 16)[None], 1, 256)
    fine_weights = (np.kron(sigma, sigma)[:, None] * fine_z).astype(np.float32)
    node_weights = (np.kron(rho, rho)[:, None] * np.tile(rho, 16)[None, :]).astype(np.float32)
    return (
        right_table(forward_z),
        left_table(grad_xy),
        left_table(interp_xy),
        left_table(back_12),
        left_table(back_3),
        left_table(back_grad),
        right_table(back_z),
        fine_weights,
        node_weights,
    )


def split(value):
    high = value.astype(BF16)
    low = (value - high.astype(F32)).astype(BF16)
    return high, low


def mm(a, b):
    return jnp.dot(a, b, preferred_element_type=F32)


def stack_rows(value):
    high, low = split(value)
    return jnp.concatenate([high, low, high], axis=0)


def stack_lanes(value):
    high, low = split(value)
    return jnp.concatenate([high, low, high], axis=1)


def kernel(n_span, n_col, *refs):
    (adj_h, base_h, md_h, mc_h, jac_h) = refs[:5]
    consts_h = refs[5:14]
    out_h = refs[14]
    (v_s, b_s, j_s, md_s, mc_s) = refs[15:20]
    consts = refs[20:29]
    (wzf, gxy_t, jxy_t, c12_t, c3_t, dxyb_t, wzb, o3, w3) = consts
    (uw_s, gw_s, o_s, xs0, xr0, xs1, xr1, zs, zr) = refs[29:38]
    (load_sem, out_sem, send_sem, recv_sem) = refs[38:]

    span = lax.axis_index("span")
    col = lax.axis_index("col")
    right, left = lax.rem(span + 1, n_span), lax.rem(span + n_span - 1, n_span)
    up, down = lax.rem(col + 1, n_col), lax.rem(col + n_col - 1, n_col)
    x_peers = ((right, col), (left, col))
    z_peers = (
        (span, up),
        (span, down),
        (right, up),
        (right, down),
        (left, up),
        (left, down),
    )

    loads = []
    for e in range(2):
        half = pl.ds(8 * e, 8)
        loads.append((base_h.at[:, :, half, :], b_s.at[:, e]))
        loads.append((adj_h.at[:, :, half, :], v_s.at[:, e]))
        loads.append((jac_h.at[:, half, :], j_s.at[e]))
    loads.append((md_h, md_s))
    loads.append((mc_h, mc_s))
    loads.extend(zip(consts_h, consts))
    copies = [
        pltpu.make_async_copy(source, target, load_sem.at[i])
        for i, (source, target) in enumerate(loads)
    ]
    for copy in copies:
        copy.start()
    barrier = pltpu.get_barrier_semaphore()
    for peer in x_peers + z_peers:
        pl.semaphore_signal(barrier, inc=1, device_id=peer, device_id_type=MESH)
    for copy in copies:
        copy.wait()

    for d in range(3):
        lines = mm(stack_lanes(b_s[d].reshape(128, 128)), wzf[:, 128:])
        for e in range(2):
            fine = mm(jxy_t[...], stack_rows(lines[64 * e : 64 * e + 64]))
            uw_s[d, e] = fine * o3[...]

    for i in range(3):
        for name, slot in ((md_s, i), (mc_s, 3 + i)):
            plane = name[i].astype(F32)
            for e in range(2):
                part = plane[:, 8 * e : 8 * e + 8, :].reshape(64, 128)
                gw_s[slot, e] = part * (VISCOSITY * w3[...])

    def pair(i, j):
        return i if i == j else 2 + i + j

    def apply_operator(field):
        high, low = split(field)
        lanes = [slice(128 * c, 128 * c + 128) for c in range(3)]
        stacked = jnp.concatenate(
            [jnp.concatenate([high[:, k], low[:, k], high[:, k]], axis=1) for k in lanes], axis=0
        )
        forward = mm(stacked, wzf[...])
        outputs = []
        for e in range(2):
            rows = slice(64 * e, 64 * e + 64)
            planes = jnp.concatenate([high[rows], low[rows], high[rows]], axis=0)
            grads = mm(gxy_t[...], planes)
            flux = [[None] * 3 for _ in range(3)]
            for c in range(3):
                g = (
                    grads[:64, lanes[c]],
                    grads[64:, lanes[c]],
                    forward[128 * c + 64 * e : 128 * c + 64 * e + 64, :128],
                )
                for d in range(3):
                    flux[d][c] = (
                        gw_s[pair(d, 0), e] * g[0]
                        + gw_s[pair(d, 1), e] * g[1]
                        + gw_s[pair(d, 2), e] * g[2]
                    )
            planar = jnp.concatenate(
                [jnp.concatenate(flux[0], axis=1), jnp.concatenate(flux[1], axis=1)], axis=0
            )
            planar_back = mm(dxyb_t[...], stack_rows(planar))
            for c in range(3):
                lines = forward[128 * c + 64 * e : 128 * c + 64 * e + 64, 128:]
                fine = mm(jxy_t[...], stack_rows(lines))
                first = jnp.concatenate([uw_s[0, e] * fine, uw_s[1, e] * fine], axis=0)
                back_12 = mm(c12_t[...], stack_rows(first))
                back_3 = mm(c3_t[...], stack_rows(uw_s[2, e] * fine))
                gathered = jnp.concatenate([back_12, back_3, flux[2][c]], axis=1)
                normal = mm(stack_lanes(gathered), wzb[...])
                outputs.append(normal + planar_back[:, lanes[c]])
        return jnp.concatenate(
            [
                jnp.concatenate(outputs[:3], axis=1),
                jnp.concatenate(outputs[3:], axis=1),
            ],
            axis=0,
        )

    def local_sum(value):
        width = value.shape[1]
        first = value[:64].reshape(8, 8, width)
        second = value[64:].reshape(8, 8, width)
        place = lax.broadcasted_iota(jnp.int32, (8, 8, width), 1)

        def plus(own, other):
            before = pltpu.roll(other, 1, 1)
            after = pltpu.roll(other, 7, 1)
            return own + jnp.where(place == 7, after, jnp.where(place == 0, before, 0.0))

        total = jnp.concatenate(
            [
                plus(first, second).reshape(64, width),
                plus(second, first).reshape(64, width),
            ],
            axis=0,
        )
        lane = lax.broadcasted_iota(jnp.int32, (128, 128), 1)
        low = (lane % 8 == 0) & (lane > 0)
        high = (lane % 8 == 7) & (lane < 127)
        pieces = []
        for c in range(width // 128):
            piece = total[:, 128 * c : 128 * c + 128]
            pieces.append(
                piece
                + jnp.where(
                    high, pltpu.roll(piece, 127, 1), jnp.where(low, pltpu.roll(piece, 1, 1), 0.0)
                )
            )
        return jnp.concatenate(pieces, axis=1)

    row = lax.broadcasted_iota(jnp.int32, (8, 512), 0)
    lane = lax.broadcasted_iota(jnp.int32, (8, 512), 1)
    ends = ((row < 4) & (lane == 128 * row)) | ((row >= 4) & (lane == 128 * (row - 4) + 127))
    ends = ends.astype(F32).astype(BF16)

    def exchange(phase, value, xs, xr):
        width = value.shape[1]
        picks = ends[:, :width]
        high, low = split(value)
        for e in range(2):
            xs[0, 8 * e : 8 * e + 8] = value[64 * e + 56 : 64 * e + 64]
            xs[1, 8 * e : 8 * e + 8] = value[64 * e : 64 * e + 8]
        contract = (((1,), (1,)), ((), ()))
        zs[phase] = lax.dot_general(
            picks, high, contract, preferred_element_type=F32
        ) + lax.dot_general(picks, low, contract, preferred_element_type=F32)
        sends = []
        for i, peer in enumerate(x_peers):
            sends.append(
                pltpu.make_async_remote_copy(
                    src_ref=xs.at[i],
                    dst_ref=xr.at[i],
                    send_sem=send_sem.at[phase, i],
                    recv_sem=recv_sem.at[phase, i],
                    device_id=peer,
                    device_id_type=MESH,
                )
            )
        for i, peer in enumerate(z_peers):
            sends.append(
                pltpu.make_async_remote_copy(
                    src_ref=zs.at[phase],
                    dst_ref=zr.at[phase, i],
                    send_sem=send_sem.at[phase, 2 + i],
                    recv_sem=recv_sem.at[phase, 2 + i],
                    device_id=peer,
                    device_id_type=MESH,
                )
            )
        for copy in sends:
            copy.start()
        return sends

    def gather(phase, value, xr, sends):
        width = value.shape[1]
        for copy in sends:
            copy.wait()
        pieces = []
        for e in range(2):
            pieces.append(value[64 * e : 64 * e + 8] + xr[0, 8 * e : 8 * e + 8])
            pieces.append(value[64 * e + 8 : 64 * e + 56])
            pieces.append(value[64 * e + 56 : 64 * e + 64] + xr[1, 8 * e : 8 * e + 8])
        total = jnp.concatenate(pieces, axis=0)
        side = lax.broadcasted_iota(jnp.int32, (8, 128), 0)
        place = lax.broadcasted_iota(jnp.int32, (8, 128), 1) % 64
        from_down = (side >= 4) & (col > 0)
        from_up = (side < 4) & (col < n_col - 1)

        def choose(below, above):
            return jnp.where(
                from_down, zr[phase, below], jnp.where(from_up, zr[phase, above], 0.0)
            )

        lines = choose(0, 1)
        lines = lines + jnp.where(place < 8, pltpu.roll(choose(2, 3), 72, 1), 0.0)
        lines = lines + jnp.where(place >= 56, pltpu.roll(choose(4, 5), 56, 1), 0.0)
        lines = pltpu.roll(lines, 4, 0)
        columns = jnp.transpose(jnp.concatenate([lines] * 16, axis=0))[:, :8]
        high, low = split(columns)
        picks = ends[:, :width]
        return total + (mm(high, picks) + mm(low, picks))

    lane = lax.broadcasted_iota(jnp.int32, (1, 128), 1)
    wall = ((lane == 0) & (col == 0)) | ((lane == 127) & (col == n_col - 1))
    interior = jnp.where(wall, 0.0, 1.0).astype(F32)

    def field_at(c):
        return v_s[c].reshape(128, 128)

    start = jnp.concatenate([field_at(c) for c in range(3)], axis=1)
    mass = jnp.concatenate([j_s[e].reshape(64, 128) * w3[...] for e in range(2)], axis=0)
    first = local_sum(jnp.concatenate([apply_operator(start), mass], axis=1))
    pl.semaphore_wait(barrier, 8)
    sends = exchange(0, first, xs0, xr0)
    total = gather(0, first, xr0, sends)
    inverse = 1.0 / total[:, 384:]
    half = jnp.concatenate(
        [
            interior
            * (
                start[:, 128 * c : 128 * c + 128]
                - (0.5 * STEP_SIZE) * inverse * total[:, 128 * c : 128 * c + 128]
            )
            for c in range(3)
        ],
        axis=1,
    )
    second = local_sum(apply_operator(half))
    sends = exchange(1, second, xs1, xr1)
    total = gather(1, second, xr1, sends)
    for c in range(3):
        result = interior * (
            field_at(c) - STEP_SIZE * inverse * total[:, 128 * c : 128 * c + 128]
        )
        o_s[c] = result.reshape(2, 8, 8, 128)
    stores = [
        pltpu.make_async_copy(o_s.at[:, e], out_h.at[:, :, pl.ds(8 * e, 8), :], out_sem.at[e])
        for e in range(2)
    ]
    for copy in stores:
        copy.start()
    for copy in stores:
        copy.wait()


def local(n_span, n_col, adjoint_field, base_flow, metric_diag, metric_cross, jacobian):
    consts = operator_tables()
    const_scratch = [pltpu.VMEM(member.shape, jnp.dtype(member.dtype)) for member in consts]
    return pl.pallas_call(
        functools.partial(kernel, n_span, n_col),
        out_shape=jax.ShapeDtypeStruct(adjoint_field.shape, F32),
        in_specs=[pl.BlockSpec(memory_space=pl.ANY)] * 14,
        out_specs=pl.BlockSpec(memory_space=pl.ANY),
        scratch_shapes=[
            pltpu.VMEM((3, 2, 8, 8, 128), F32),
            pltpu.VMEM((3, 2, 8, 8, 128), F32),
            pltpu.VMEM((2, 8, 8, 128), F32),
            pltpu.VMEM((3, 8, 16, 128), BF16),
            pltpu.VMEM((3, 8, 16, 128), BF16),
            *const_scratch,
            pltpu.VMEM((3, 2, 144, 256), F32),
            pltpu.VMEM((6, 2, 64, 128), F32),
            pltpu.VMEM((3, 2, 8, 8, 128), F32),
            pltpu.VMEM((2, 16, 512), F32),
            pltpu.VMEM((2, 16, 512), F32),
            pltpu.VMEM((2, 16, 384), F32),
            pltpu.VMEM((2, 16, 384), F32),
            pltpu.VMEM((2, 8, 128), F32),
            pltpu.VMEM((2, 6, 8, 128), F32),
            pltpu.SemaphoreType.DMA((17,)),
            pltpu.SemaphoreType.DMA((2,)),
            pltpu.SemaphoreType.DMA((2, 8)),
            pltpu.SemaphoreType.DMA((2, 8)),
        ],
        compiler_params=pltpu.CompilerParams(collective_id=0, has_side_effects=True),
    )(
        adjoint_field,
        base_flow,
        metric_diag,
        metric_cross,
        jacobian,
        *[jnp.asarray(member) for member in consts],
    )


def solution(mesh):
    in_specs = (
        P(None, "span", None, "col"),
        P(None, "span", None, "col"),
        P(None, "span", None, "col"),
        P(None, "span", None, "col"),
        P("span", None, "col"),
    )
    out_specs = P(None, "span", None, "col")
    body = functools.partial(local, mesh.shape["span"], mesh.shape["col"])
    return jax.shard_map(body, mesh=mesh, in_specs=in_specs, out_specs=out_specs, check_vma=False)
```

time: 126 us -> 41.7 us (0.33)
  starting transfers between devices: 45 us -> 0 us
  Pallas kernels: 0 us -> 39.9 us
  matrix products: 33.1 us -> 0 us
  waiting for transfers between devices: 23.4 us -> 0 us
  local copies, waits for them, and re-layouts: 17 us -> 1.62 us
  other arithmetic: 5.19 us -> 0 us
    ppermute x8 -> x0, starting transfers between devices: 45 us -> none  [the longest x4 24.7 us: padded_2(): lax.ppermute(lax.slice_in_dim(block, 0, width, axis=dim), axis, backward)]
    pallas_call x0 -> x1, Pallas kernels: none -> 39.9 us  [local(): pl.pallas_call(functools.partial(kernel, n_span, n_col), out_shape=jax.Sh...]
    dot_general x39 -> x0, matrix products: 33.1 us -> none  [the longest x13 17.9 us: along_third(): result = jnp.einsum('lxyzk,kq->lxyzq', blocks, kron_table, precision=HIGH)]
    ppermute x8 -> x0, waiting for transfers between devices: 23.4 us -> none  [the longest x4 19.9 us: padded_2(): lax.ppermute(lax.slice_in_dim(block, block.shape[dim] - width, None, axis...]
    mul x17 -> x0, local copies, waits for them, and re-layouts: 7.72 us -> none  [the longest x5 3.68 us: along_third(): kron_table = jnp.kron(jnp.eye(group_size, dtype=jnp.float32), matrix.T)]
    another operation x7 -> x0, local copies, waits for them, and re-layouts: 4.33 us -> none
    mul x12 -> x0, other arithmetic: 4.28 us -> none  [the longest x3 2.14 us: weight_grid(): first_axis[:, None, None] * second_axis[None, :, None]]
    dot_general x6 -> x0, local copies, waits for them, and re-layouts: 2.91 us -> none  [along_third(): result = jnp.einsum('lxyzk,kq->lxyzq', blocks, kron_table, precision=HIGH)]
  transfers between devices with their start and end apart: 8 -> 0, of which waited for: 6 -> 0; matrix products, arithmetic and copies ran while one was open for 0% -> 0% of each run, Pallas kernels for 0% -> 0%
where the time goes in v1:
time: 41.7 us; the launch traced here: 41.5 us
  Pallas kernels  39.9 us (96%)
  local copies, waits for them, and re-layouts  1.62 us (4%)
    pallas_call x1, Pallas kernels, local(): pl.pallas_call(functools.partial(kernel, n_span, n_col), out_shape=jax.Sh...  39.9 us
    unnamed x1, local copies, waits for them, and re-layouts  1.62 us

profile of v1, /device:TPU:1, one launch (start us, length us, event | category | flops | bytes accessed | tf_op | source)
XLA Modules:
  0.0 41.5 jit_solution(14223163777663700621)
XLA Ops:
  0.0 39.9 %shard_map.136 = f32[3,8,16,128]{3,2,1,0:T(8,128)} custom-call(f32[3,8,16,128]{3,2,1,0:T(8,128)} %refs_0_.1, f32[3,8,16,128]{3,2,1,0:T(8,128)} %refs_1_.1, bf16[3,8,16,128]{3,2,1,0:T(8,128)(2,1)} %refs_2_.1, bf16[3,8,16,128]{3,2,1,0:T(8,128)(2,1)} %refs_3_.1, f32[8,16,128]{2,1,0:T(8,128)} %refs_4_.1, bf16[384,384]{1,0:T(8,128)(2,1)} %constant.18.clone.refs_5_, ...), custom_call_target="tpu_custom_call" | custom-call | tf_op jit(solution)/shard_map/pallas_call | solution.py:421
  39.9 1.6 %copy.16 = f32[3,8,16,128]{3,2,1,0:T(8,128)} copy(f32[3,8,16,128]{3,2,1,0:T(8,128)} %shard_map.136) | data formatting | bytes 393216

commit v2 on v1

v2 whole, which is shorter than its diff:
```python
import functools

import jax
import jax.numpy as jnp
import ml_dtypes
import numpy as np
from jax import lax
from jax.experimental import pallas as pl
from jax.experimental.pallas import tpu as pltpu
from jax.sharding import PartitionSpec as P

VISCOSITY = 0.05
STEP_SIZE = 0.01
GLL_INNER = [
    -0.8717401485096066,
    -0.5917001814331423,
    -0.2092992179024789,
    0.2092992179024789,
    0.5917001814331423,
    0.8717401485096066,
]
GAUSS_POINTS = [
    -0.9815606342467192,
    -0.9041172563704749,
    -0.7699026741943047,
    -0.5873179542866175,
    -0.3678314989981802,
    -0.1252334085114689,
    0.1252334085114689,
    0.3678314989981802,
    0.5873179542866175,
    0.7699026741943047,
    0.9041172563704749,
    0.9815606342467192,
]
GAUSS_WEIGHTS = [
    0.0471753363865118,
    0.1069393259953184,
    0.1600783285433462,
    0.2031674267230659,
    0.2334925365383548,
    0.2491470458134028,
    0.2491470458134028,
    0.2334925365383548,
    0.2031674267230659,
    0.1600783285433462,
    0.1069393259953184,
    0.0471753363865118,
]
MESH = pl.DeviceIdType.MESH
F32 = jnp.float32
BF16 = jnp.bfloat16


def legendre_seven(points):
    previous = points * 0.0 + 1.0
    current = points
    for degree in range(1, 7):
        following = ((2.0 * degree + 1.0) * points * current - degree * previous) / (degree + 1.0)
        previous = current
        current = following
    return current


def node_tables():
    gll_nodes = np.array([-1.0] + GLL_INNER + [1.0])
    values = legendre_seven(gll_nodes)
    node_weights = 2.0 / (56.0 * values * values)
    identity = np.eye(8, dtype=bool)
    spacing = gll_nodes[:, None] - gll_nodes[None, :]
    derivative = np.where(
        identity, 0.0, values[:, None] / (values[None, :] * np.where(identity, 1.0, spacing))
    )
    corner_terms = np.concatenate([np.array([-14.0]), np.zeros(6), np.array([14.0])])
    derivative = derivative + np.eye(8) * corner_terms[None, :]
    gauss_nodes = np.array(GAUSS_POINTS)
    gauss_weights = np.array(GAUSS_WEIGHTS)
    numerators = gauss_nodes[:, None, None] - gll_nodes[None, None, :]
    denominators = np.where(identity, 1.0, spacing)[None]
    ratios = np.where(identity[None], 1.0, numerators / denominators)
    interpolation = ratios.prod(axis=2)
    slope_interp = interpolation @ derivative
    return tuple(
        np.asarray(member, np.float32).astype(np.float64)
        for member in (derivative, node_weights, interpolation, slope_interp, gauss_weights)
    )


def halves(matrix):
    high = matrix.astype(np.float32).astype(ml_dtypes.bfloat16)
    low = (matrix - high.astype(np.float64)).astype(np.float32).astype(ml_dtypes.bfloat16)
    return high, low


def left_table(matrix):
    return np.concatenate([halves(matrix)[i] for i in (0, 0, 1)], axis=1)


def right_table(matrix):
    return np.stack(halves(matrix))


def operator_tables():
    dm, rho, jm, dj, sigma = node_tables()
    eye8, eye16 = np.eye(8), np.eye(16)
    ends_lanes = [(c, 15 * s, (2 * c + s) * 12) for c in range(3) for s in range(2)]
    middle_lanes = [(0, a, (a - 1) * 12) for a in range(1, 15)]
    middle_lanes += [(1, a, (13 + a) * 12) for a in range(1, 8)]

    def lines(matrix, lanes, components, width):
        table = np.zeros((components * 128, width))
        for c, a, lane in lanes:
            table[128 * c + 8 * a : 128 * c + 8 * a + 8, lane : lane + 12] = matrix.T
        return table

    flow = np.zeros((128, 640))
    weights_z = np.zeros((1, 640))
    for tile, lanes in enumerate((ends_lanes, middle_lanes, middle_lanes)):
        for c, a, lane in lanes:
            start = lane + (0, 128, 384)[tile]
            element = a + 7 if tile == 2 and c == 1 else a
            flow[8 * element : 8 * element + 8, start : start + 12] = jm.T
            weights_z[0, start : start + 12] = sigma
    weights_xy = np.broadcast_to(np.kron(sigma, sigma)[:, None], (144, 128)).astype(np.float32)
    weights_z = np.broadcast_to(weights_z, (8, 640)).astype(np.float32)
    node_weights = (np.kron(rho, rho)[:, None] * np.tile(rho, 16)[None, :]).astype(np.float32)
    back_ends = np.concatenate(
        [lines(jm, ends_lanes, 3, 128).T, lines(dj, ends_lanes, 3, 128).T], axis=0
    )
    back_middle = np.concatenate(
        [lines(jm, middle_lanes, 2, 256).T, lines(dj, middle_lanes, 2, 256).T], axis=0
    )
    return (
        right_table(np.kron(eye16, dm.T)),
        right_table(np.kron(eye16, dm)),
        left_table(np.concatenate([np.kron(dm, eye8), np.kron(eye8, dm)], axis=0)),
        left_table(np.concatenate([np.kron(dm.T, eye8), np.kron(eye8, dm.T)], axis=1)),
        right_table(flow),
        right_table(lines(jm, ends_lanes, 3, 128)),
        right_table(lines(jm, middle_lanes, 2, 256)),
        left_table(np.kron(jm, jm)),
        left_table(np.concatenate([np.kron(dj.T, jm.T), np.kron(jm.T, dj.T)], axis=1)),
        left_table(np.kron(jm.T, jm.T)),
        right_table(back_ends),
        right_table(back_middle),
        weights_xy,
        weights_z,
        node_weights,
    )


def split(value):
    high = value.astype(BF16)
    low = (value - high.astype(F32)).astype(BF16)
    return high, low


def mm(a, b):
    return jnp.dot(a, b, preferred_element_type=F32)


def mm_right(stacked, table):
    return mm(stacked, jnp.concatenate([table[0], table[0], table[1]], axis=0))


def stack_rows(value):
    high, low = split(value)
    return jnp.concatenate([high, low, high], axis=0)


def stack_lanes(value):
    high, low = split(value)
    return jnp.concatenate([high, low, high], axis=1)


def kernel(n_span, n_col, *refs):
    (adj_h, base_h, md_h, mc_h, jac_h) = refs[:5]
    consts_h = refs[5:20]
    out = refs[20]
    (v_s, b_s, j_s, md_s, mc_s) = refs[21:26]
    consts = refs[26:41]
    (wg, wgb, gxy, gxyb, wflow, wfe, wfm, jxy, c12, c3, wbe, wbm, o_xy, o_z, w3) = consts
    (uw_s, gw_s, xs0, xr0, xs1, xr1, zs, zr, rs, rr) = refs[41:51]
    (load_sem, send_sem, recv_sem) = refs[51:]

    span = lax.axis_index("span")
    col = lax.axis_index("col")
    right, left = lax.rem(span + 1, n_span), lax.rem(span + n_span - 1, n_span)
    up, down = lax.rem(col + 1, n_col), lax.rem(col + n_col - 1, n_col)
    x_peers = ((right, col), (left, col))
    z_peers = ((span, up), (span, down))

    tables = list(zip(consts_h, consts))
    y_halves = [pl.ds(0, 8), pl.ds(8, 8)]
    groups = [
        [(base_h.at[:, :, y_halves[e], :], b_s.at[:, e]) for e in range(2)]
        + [tables[i] for i in (4, 7, 12, 13)],
        [(md_h, md_s), (mc_h, mc_s), tables[14]]
        + [(adj_h.at[:, :, y_halves[e], :], v_s.at[:, e]) for e in range(2)]
        + [(jac_h.at[:, y_halves[e], :], j_s.at[e]) for e in range(2)]
        + tables[:4],
        [tables[i] for i in (5, 8, 9, 10)],
        [tables[i] for i in (6, 11)],
    ]
    loads, used = [], 0
    for group in groups:
        loads.append(
            [
                pltpu.make_async_copy(source, target, load_sem.at[used + i])
                for i, (source, target) in enumerate(group)
            ]
        )
        used += len(group)
    for group in loads:
        for copy in group:
            copy.start()

    def arrive(group):
        for copy in loads[group]:
            copy.wait()

    barrier = pltpu.get_barrier_semaphore()
    for peer in x_peers + z_peers:
        pl.semaphore_signal(barrier, inc=1, device_id=peer, device_id_type=MESH)
    arrive(0)
    planes = []
    for e in range(2):
        rows = jnp.concatenate([b_s[d, e].reshape(64, 128) for d in range(3)], axis=1)
        fine = mm(jxy[...], stack_rows(rows))
        planes.extend(fine[:, 128 * d : 128 * d + 128] for d in range(3))
    fine_weights = o_xy[:, :1] * o_z[:1]
    flow = mm_right(stack_lanes(jnp.concatenate(planes, axis=0)), wflow)
    for e in range(2):
        for d in range(3):
            first = 144 * (3 * e + d)
            uw_s[d, e] = flow[first : first + 144] * fine_weights

    arrive(1)
    for i in range(3):
        for name, slot in ((md_s, i), (mc_s, 3 + i)):
            plane = name[i].astype(F32)
            for e in range(2):
                part = plane[:, 8 * e : 8 * e + 8, :].reshape(64, 128)
                gw_s[slot, e] = part * (VISCOSITY * w3[...])

    lanes = [slice(128 * c, 128 * c + 128) for c in range(4)]
    halves_of = [slice(0, 64), slice(64, 128)]

    def pair(i, j):
        return i if i == j else 2 + i + j

    def stiffness(high, low):
        stacked = jnp.concatenate(
            [jnp.concatenate([high[c], low[c], high[c]], axis=1) for c in range(3)], axis=0
        )
        grad_z = mm_right(stacked, wg)
        planar, fluxes = [], [[None, None] for _ in range(3)]
        for e in range(2):
            wide_high = jnp.concatenate([high[c][halves_of[e]] for c in range(3)], axis=1)
            wide_low = jnp.concatenate([low[c][halves_of[e]] for c in range(3)], axis=1)
            grads = mm(gxy[...], jnp.concatenate([wide_high, wide_low, wide_high], axis=0))
            flux = [[None] * 3 for _ in range(2)]
            for c in range(3):
                start = 128 * c + 64 * e
                g = (
                    grads[:64, lanes[c]],
                    grads[64:, lanes[c]],
                    grad_z[start : start + 64],
                )
                h = [
                    gw_s[pair(d, 0), e] * g[0]
                    + gw_s[pair(d, 1), e] * g[1]
                    + gw_s[pair(d, 2), e] * g[2]
                    for d in range(3)
                ]
                flux[0][c], flux[1][c], fluxes[c][e] = h
            joined = jnp.concatenate([jnp.concatenate(f, axis=1) for f in flux], axis=0)
            planar.append(mm(gxyb[...], stack_rows(joined)))
        normal = mm_right(
            stack_lanes(jnp.concatenate([f for two in fluxes for f in two], axis=0)), wgb
        )
        return jnp.concatenate(planar, axis=0) + jnp.concatenate(
            [normal[128 * c : 128 * c + 128] for c in range(3)], axis=1
        )

    def convection(lines, window):
        pieces = []
        for e in range(2):
            fine = mm(jxy[...], stack_rows(lines[halves_of[e]]))
            planar = jnp.concatenate([uw_s[d, e, :, window] * fine for d in range(2)], axis=0)
            pieces.append(
                (
                    mm(c12[...], stack_rows(planar)),
                    mm(c3[...], stack_rows(uw_s[2, e, :, window] * fine)),
                )
            )
        return pieces

    def end_convection(high, low):
        stacked = jnp.concatenate(high + low + high, axis=1)
        pieces = convection(mm_right(stacked, wfe), slice(0, 128))
        joined = jnp.concatenate([jnp.concatenate(p, axis=1) for p in pieces], axis=0)
        return mm_right(stack_lanes(joined), wbe)

    def middle_convection(field, high, low):
        shifted_high, shifted_low = split(pltpu.roll(field[2], 72, 1))
        stacked = jnp.concatenate(
            [
                jnp.concatenate([high[0], high[2], low[0], low[2], high[0], high[2]], axis=1),
                jnp.concatenate(
                    [high[1], shifted_high, low[1], shifted_low, high[1], shifted_high], axis=1
                ),
            ],
            axis=0,
        )
        both = mm_right(stacked, wfm)
        lines = jnp.concatenate([both[:128], both[128:]], axis=1)
        pieces = convection(lines, slice(128, 640))
        joined = jnp.concatenate(
            [
                jnp.concatenate([part[:, 256 * t : 256 * t + 256] for part in pieces[e]], axis=1)
                for t in range(2)
                for e in range(2)
            ],
            axis=0,
        )
        back = mm_right(stack_lanes(joined), wbm)
        tail = back[:128, 128:] + pltpu.roll(back[128:, 128:], 56, 1)
        return jnp.concatenate([back[:128, :128], back[128:, :128], tail], axis=1)

    def local_sum(value, low, high):
        width, count = value.shape[1], high - low
        two = [value[64 * e + 8 * low : 64 * e + 8 * high] for e in range(2)]
        two = [member.reshape(count, 8, width) for member in two]
        place = lax.broadcasted_iota(jnp.int32, (count, 8, width), 1)
        lane = lax.broadcasted_iota(jnp.int32, (8 * count, 128), 1)
        begins = (lane % 8 == 0) & (lane > 0)
        closes = (lane % 8 == 7) & (lane < 127)
        results = []
        for own, other in ((two[0], two[1]), (two[1], two[0])):
            before = pltpu.roll(other, 1, 1)
            after = pltpu.roll(other, 7, 1)
            total = own + jnp.where(place == 7, after, jnp.where(place == 0, before, 0.0))
            total = total.reshape(8 * count, width)
            pieces = []
            for c in range(width // 128):
                piece = total[:, lanes[c]]
                near = jnp.where(
                    closes,
                    pltpu.roll(piece, 127, 1),
                    jnp.where(begins, pltpu.roll(piece, 1, 1), 0.0),
                )
                pieces.append(piece + near)
            results.append(jnp.concatenate(pieces, axis=1))
        return results

    row = lax.broadcasted_iota(jnp.int32, (8, 512), 0)
    lane = lax.broadcasted_iota(jnp.int32, (8, 512), 1)
    ends = ((row < 4) & (lane == 128 * row)) | ((row >= 4) & (lane == 128 * (row - 4) + 127))
    ends = ends.astype(F32).astype(BF16)
    side = lax.broadcasted_iota(jnp.int32, (8, 128), 0)
    place = lax.broadcasted_iota(jnp.int32, (8, 128), 1) % 64

    def remote(source, target, phase, i, peer):
        return pltpu.make_async_remote_copy(
            src_ref=source,
            dst_ref=target,
            send_sem=send_sem.at[phase, i],
            recv_sem=recv_sem.at[phase, i],
            device_id=peer,
            device_id_type=MESH,
        )

    def send_ends(phase, value):
        width = value.shape[1]
        high, low = split(value)
        contract = (((1,), (1,)), ((), ()))
        tile = lax.dot_general(
            ends[:, :width], high, contract, preferred_element_type=F32
        ) + lax.dot_general(ends[:, :width], low, contract, preferred_element_type=F32)
        after = jnp.where(place % 8 == 7, pltpu.roll(tile, 71, 1), 0.0)
        before = jnp.where(place % 8 == 0, pltpu.roll(tile, 57, 1), 0.0)
        zs[phase] = tile + after + before
        copies = [
            remote(zs.at[phase], zr.at[phase, i], phase, 2 + i, peer)
            for i, peer in enumerate(z_peers)
        ]
        for copy in copies:
            copy.start()
        return copies

    def exchange(phase, value, xs, xr, z_copies):
        faces = [local_sum(value, 7, 8), local_sum(value, 0, 1)]
        for i in range(2):
            for e in range(2):
                xs[i, 8 * e : 8 * e + 8] = faces[i][e]
        x_copies = [
            remote(xs.at[i], xr.at[i], phase, i, peer) for i, peer in enumerate(x_peers)
        ]
        for copy in x_copies:
            copy.start()
        inner = local_sum(value, 1, 7)
        for copy in z_copies:
            copy.wait_recv()
        from_down = (side >= 4) & (col > 0)
        from_up = (side < 4) & (col < n_col - 1)
        lines = jnp.where(from_down, zr[phase, 0], jnp.where(from_up, zr[phase, 1], 0.0))
        rs[phase] = lines
        relays = [
            remote(rs.at[phase], rr.at[phase, i], phase, 4 + i, peer)
            for i, peer in enumerate(x_peers)
        ]
        for copy in relays:
            copy.start()
        for copy in x_copies + relays:
            copy.wait_recv()
        lines = lines + jnp.where(place < 8, pltpu.roll(rr[phase, 0], 72, 1), 0.0)
        lines = lines + jnp.where(place >= 56, pltpu.roll(rr[phase, 1], 56, 1), 0.0)
        lines = pltpu.roll(lines, 4, 0)
        columns = jnp.transpose(jnp.concatenate([lines] * 16, axis=0))[:, :8]
        high, low = split(columns)
        picks = ends[:, : value.shape[1]]
        pieces = []
        for e in range(2):
            pieces.append(faces[1][e] + xr[0, 8 * e : 8 * e + 8])
            pieces.append(inner[e])
            pieces.append(faces[0][e] + xr[1, 8 * e : 8 * e + 8])
        total = jnp.concatenate(pieces, axis=0) + (mm(high, picks) + mm(low, picks))
        for copy in x_copies + z_copies + relays:
            copy.wait_send()
        return total

    lane = lax.broadcasted_iota(jnp.int32, (1, 128), 1)
    wall = ((lane == 0) & (col == 0)) | ((lane == 127) & (col == n_col - 1))
    interior = jnp.where(wall, 0.0, 1.0).astype(F32)

    start = [v_s[c].reshape(128, 128) for c in range(3)]
    mass = jnp.concatenate([j_s[e].reshape(64, 128) * w3[...] for e in range(2)], axis=0)

    pairs = [split(member) for member in start]
    high, low = [p[0] for p in pairs], [p[1] for p in pairs]
    value = stiffness(high, low)
    arrive(2)
    value = jnp.concatenate([value + end_convection(high, low), mass], axis=1)
    pl.semaphore_wait(barrier, 4)
    z_copies = send_ends(0, value)
    arrive(3)
    middle = middle_convection(start, high, low)
    value = jnp.concatenate([value[:, :384] + middle, mass], axis=1)
    total = exchange(0, value, xs0, xr0, z_copies)
    inverse = 1.0 / total[:, lanes[3]]
    half = [
        interior * (start[c] - (0.5 * STEP_SIZE) * inverse * total[:, lanes[c]]) for c in range(3)
    ]

    pairs = [split(member) for member in half]
    high, low = [p[0] for p in pairs], [p[1] for p in pairs]
    value = stiffness(high, low) + end_convection(high, low)
    z_copies = send_ends(1, value)
    value = value + middle_convection(half, high, low)
    total = exchange(1, value, xs1, xr1, z_copies)
    for c in range(3):
        result = interior * (
            v_s[c].reshape(128, 128) - STEP_SIZE * inverse * total[:, lanes[c]]
        )
        for e in range(2):
            out[c, :, 8 * e : 8 * e + 8, :] = result[halves_of[e]].reshape(8, 8, 128)


def local(n_span, n_col, adjoint_field, base_flow, metric_diag, metric_cross, jacobian):
    consts = operator_tables()
    const_scratch = [pltpu.VMEM(member.shape, jnp.dtype(member.dtype)) for member in consts]
    return pl.pallas_call(
        functools.partial(kernel, n_span, n_col),
        out_shape=pltpu.VMEM(adjoint_field.shape, F32),
        in_specs=[pl.BlockSpec(memory_space=pl.ANY)] * 20,
        out_specs=pl.BlockSpec(memory_space=pltpu.VMEM),
        scratch_shapes=[
            pltpu.VMEM((3, 2, 8, 8, 128), F32),
            pltpu.VMEM((3, 2, 8, 8, 128), F32),
            pltpu.VMEM((2, 8, 8, 128), F32),
            pltpu.VMEM((3, 8, 16, 128), BF16),
            pltpu.VMEM((3, 8, 16, 128), BF16),
            *const_scratch,
            pltpu.VMEM((3, 2, 144, 640), F32),
            pltpu.VMEM((6, 2, 64, 128), F32),
            pltpu.VMEM((2, 16, 512), F32),
            pltpu.VMEM((2, 16, 512), F32),
            pltpu.VMEM((2, 16, 384), F32),
            pltpu.VMEM((2, 16, 384), F32),
            pltpu.VMEM((2, 8, 128), F32),
            pltpu.VMEM((2, 2, 8, 128), F32),
            pltpu.VMEM((2, 8, 128), F32),
            pltpu.VMEM((2, 2, 8, 128), F32),
            pltpu.SemaphoreType.DMA((23,)),
            pltpu.SemaphoreType.DMA((2, 6)),
            pltpu.SemaphoreType.DMA((2, 6)),
        ],
        compiler_params=pltpu.CompilerParams(collective_id=0, has_side_effects=True),
    )(
        adjoint_field,
        base_flow,
        metric_diag,
        metric_cross,
        jacobian,
        *[jnp.asarray(member) for member in consts],
    )


def solution(mesh):
    in_specs = (
        P(None, "span", None, "col"),
        P(None, "span", None, "col"),
        P(None, "span", None, "col"),
        P(None, "span", None, "col"),
        P("span", None, "col"),
    )
    out_specs = P(None, "span", None, "col")
    body = functools.partial(local, mesh.shape["span"], mesh.shape["col"])
    return jax.shard_map(body, mesh=mesh, in_specs=in_specs, out_specs=out_specs, check_vma=False)
```

time: 41.7 us -> 36.6 us (0.88)
  Pallas kernels: 39.9 us -> 35.8 us
  local copies, waits for them, and re-layouts: 1.62 us -> 0.68 us
    pallas_call x1, Pallas kernels: 39.9 us -> 35.8 us  [local(): pl.pallas_call(functools.partial(kernel, n_span, n_col), out_shape=pltpu....]
    unnamed x1, local copies, waits for them, and re-layouts: 1.62 us -> 0.68 us
where the time goes in v2:
time: 36.6 us; the launch traced here: 36.4 us
  Pallas kernels  35.8 us (98%)
  local copies, waits for them, and re-layouts  0.68 us (2%)
    pallas_call x1, Pallas kernels, local(): pl.pallas_call(functools.partial(kernel, n_span, n_col), out_shape=pltpu....  35.8 us

profile of v2, /device:TPU:1, one launch (start us, length us, event | category | flops | bytes accessed | tf_op | source)
XLA Modules:
  0.0 36.4 jit_solution(13387474641204748616)
XLA Ops:
  0.0 35.8 %shard_map.190 = f32[3,8,16,128]{3,2,1,0:T(8,128)S(1)} custom-call(f32[3,8,16,128]{3,2,1,0:T(8,128)} %refs_0_.1, f32[3,8,16,128]{3,2,1,0:T(8,128)} %refs_1_.1, bf16[3,8,16,128]{3,2,1,0:T(8,128)(2,1)} %refs_2_.1, bf16[3,8,16,128]{3,2,1,0:T(8,128)(2,1)} %refs_3_.1, f32[8,16,128]{2,1,0:T(8,128)} %refs_4_.1, bf16[2,128,128]{2,1,0:T(8,128)(2,1)} %constant.30.clone.refs_5_, ...), custom_call_target="tpu_custom_call" | custom-call | tf_op jit(solution)/shard_map/pallas_call | solution.py:473
  35.8 0.7 %copy.22 = f32[3,8,16,128]{3,2,1,0:T(8,128)} copy(f32[3,8,16,128]{3,2,1,0:T(8,128)S(1)} %shard_map.190) | data formatting | bytes 393216

commit v3 on v2

v3 whole, which is shorter than its diff:
```python
import functools

import jax
import jax.numpy as jnp
import ml_dtypes
import numpy as np
from jax import lax
from jax.experimental import pallas as pl
from jax.experimental.pallas import tpu as pltpu
from jax.sharding import PartitionSpec as P

VISCOSITY = 0.05
STEP_SIZE = 0.01
GLL_INNER = [
    -0.8717401485096066,
    -0.5917001814331423,
    -0.2092992179024789,
    0.2092992179024789,
    0.5917001814331423,
    0.8717401485096066,
]
GAUSS_POINTS = [
    -0.9815606342467192,
    -0.9041172563704749,
    -0.7699026741943047,
    -0.5873179542866175,
    -0.3678314989981802,
    -0.1252334085114689,
    0.1252334085114689,
    0.3678314989981802,
    0.5873179542866175,
    0.7699026741943047,
    0.9041172563704749,
    0.9815606342467192,
]
GAUSS_WEIGHTS = [
    0.0471753363865118,
    0.1069393259953184,
    0.1600783285433462,
    0.2031674267230659,
    0.2334925365383548,
    0.2491470458134028,
    0.2491470458134028,
    0.2334925365383548,
    0.2031674267230659,
    0.1600783285433462,
    0.1069393259953184,
    0.0471753363865118,
]
MESH = pl.DeviceIdType.MESH
F32 = jnp.float32
BF16 = jnp.bfloat16


def legendre_seven(points):
    previous = points * 0.0 + 1.0
    current = points
    for degree in range(1, 7):
        following = ((2.0 * degree + 1.0) * points * current - degree * previous) / (degree + 1.0)
        previous = current
        current = following
    return current


def node_tables():
    gll_nodes = np.array([-1.0] + GLL_INNER + [1.0])
    values = legendre_seven(gll_nodes)
    node_weights = 2.0 / (56.0 * values * values)
    identity = np.eye(8, dtype=bool)
    spacing = gll_nodes[:, None] - gll_nodes[None, :]
    derivative = np.where(
        identity, 0.0, values[:, None] / (values[None, :] * np.where(identity, 1.0, spacing))
    )
    corner_terms = np.concatenate([np.array([-14.0]), np.zeros(6), np.array([14.0])])
    derivative = derivative + np.eye(8) * corner_terms[None, :]
    gauss_nodes = np.array(GAUSS_POINTS)
    gauss_weights = np.array(GAUSS_WEIGHTS)
    numerators = gauss_nodes[:, None, None] - gll_nodes[None, None, :]
    denominators = np.where(identity, 1.0, spacing)[None]
    ratios = np.where(identity[None], 1.0, numerators / denominators)
    interpolation = ratios.prod(axis=2)
    slope_interp = interpolation @ derivative
    return tuple(
        np.asarray(member, np.float32).astype(np.float64)
        for member in (derivative, node_weights, interpolation, slope_interp, gauss_weights)
    )


def halves(matrix):
    high = matrix.astype(np.float32).astype(ml_dtypes.bfloat16)
    low = (matrix - high.astype(np.float64)).astype(np.float32).astype(ml_dtypes.bfloat16)
    return high, low


def left_table(matrix):
    return np.concatenate([halves(matrix)[i] for i in (0, 0, 1)], axis=1)


def right_table(matrix):
    return np.stack(halves(matrix))


def operator_tables():
    dm, rho, jm, dj, sigma = node_tables()
    eye8, eye16 = np.eye(8), np.eye(16)
    ends = [(16 * c + 8 * s, 24 * c + 12 * s) for c in range(3) for s in range(2)]
    middle = [(8 * a, 12 * (a - 1)) for a in range(1, 15)]
    middle += [(128 + 8 * a, 12 * (13 + a)) for a in range(1, 8)]

    def blocks(matrix, places, rows, columns):
        table = np.zeros((rows, columns))
        for first, second in places:
            height, width = matrix.shape
            second = second if width == 12 else first
            table[first : first + height, second : second + width] = matrix
        return table

    to_ends = np.concatenate(
        [blocks(dm.T, ends, 128, 128), blocks(jm.T, ends, 128, 128)], axis=1
    )
    from_ends = np.concatenate(
        [
            blocks(jm.T, ends, 128, 128).T,
            blocks(dj.T, ends, 128, 128).T,
            blocks(dm.T, ends, 128, 128).T,
        ],
        axis=0,
    )
    to_middle = blocks(jm.T, middle, 256, 256)
    from_middle = np.concatenate([to_middle.T, blocks(dj.T, middle, 256, 256).T], axis=0)

    flow_ends, flow_middle = np.zeros((128, 128)), np.zeros((128, 512))
    sigma_z = np.zeros((1, 512))
    for node, gauss in ends:
        element = 0 if node % 16 == 8 else 120
        flow_ends[element : element + 8, gauss : gauss + 12] = jm.T
        sigma_z[0, gauss : gauss + 12] = sigma
    for t in range(2):
        for node, gauss in middle:
            element = node if node < 128 else node - 128 + 56 * t
            flow_middle[element : element + 8, 256 * t + gauss : 256 * t + gauss + 12] = jm.T
    tile = np.zeros(256)
    for node, gauss in middle:
        tile[gauss : gauss + 12] = sigma
    sigma_z[0, 128:256], sigma_z[0, 256:384], sigma_z[0, 384:] = tile[:128], tile[128:], tile[128:]
    flow_middle = np.concatenate([flow_middle[:, :256], flow_middle[:, 384:]], axis=1)
    sigma_z = np.broadcast_to(sigma_z, (8, 512)).astype(np.float32)
    sigma_xy = np.broadcast_to(np.kron(sigma, sigma)[:, None], (144, 128)).astype(np.float32)

    node_weights = (np.kron(rho, rho)[:, None] * np.tile(rho, 16)[None, :]).astype(np.float32)
    choose_ends = np.zeros((128, 128))
    for node, _ in ends:
        element = 0 if node % 16 == 8 else 120
        choose_ends[element : element + 8, node : node + 8] = np.eye(8)
    return {
        "z_grad": right_table(np.kron(eye16, dm.T)),
        "z_grad_back": right_table(np.kron(eye16, dm)),
        "xy_grad": left_table(np.concatenate([np.kron(dm, eye8), np.kron(eye8, dm)], axis=0)),
        "xy_grad_back": left_table(
            np.concatenate([np.kron(dm.T, eye8), np.kron(eye8, dm.T)], axis=1)
        ),
        "xy_interp": left_table(np.kron(jm, jm)),
        "xy_back_12": left_table(
            np.concatenate([np.kron(dj.T, jm.T), np.kron(jm.T, dj.T)], axis=1)
        ),
        "xy_back_3": left_table(np.kron(jm.T, jm.T)),
        "to_ends": right_table(to_ends),
        "from_ends": right_table(from_ends),
        "to_middle": right_table(to_middle),
        "from_middle": right_table(from_middle),
        "flow_ends": right_table(flow_ends),
        "flow_middle": right_table(flow_middle),
        "choose_ends": choose_ends.astype(ml_dtypes.bfloat16),
        "sigma_xy": sigma_xy,
        "sigma_z": sigma_z,
        "node_weights": node_weights,
    }


def split(value):
    high = value.astype(BF16)
    low = (value - high.astype(F32)).astype(BF16)
    return high, low


def mm(a, b):
    return jnp.dot(a, b, preferred_element_type=F32)


def mm_right(stacked, table):
    return mm(stacked, jnp.concatenate([table[0], table[0], table[1]], axis=0))


def stack_rows(value):
    high, low = split(value)
    return jnp.concatenate([high, low, high], axis=0)


def stack_lanes(value):
    high, low = split(value)
    return jnp.concatenate([high, low, high], axis=1)


def kernel(n_span, n_col, names, *refs):
    n_tables = len(names)
    (adj_h, base_h, md_h, mc_h, jac_h) = refs[:5]
    tables_h = dict(zip(names, refs[5 : 5 + n_tables]))
    out = refs[5 + n_tables]
    refs = refs[6 + n_tables :]
    (v_s, b_s, j_s, md_s, mc_s) = refs[:5]
    tables = dict(zip(names, refs[5 : 5 + n_tables]))
    refs = refs[5 + n_tables :]
    (ue_s, um_s, ge_s, gw_s, xs0, xr0, xs1, xr1, zs, zr, rs, rr, dr) = refs[:13]
    (load_sem, send_sem, recv_sem) = refs[13:]

    span = lax.axis_index("span")
    col = lax.axis_index("col")
    right, left = lax.rem(span + 1, n_span), lax.rem(span + n_span - 1, n_span)
    up, down = lax.rem(col + 1, n_col), lax.rem(col + n_col - 1, n_col)
    x_peers = ((right, col), (left, col))
    z_peers = ((span, up), (span, down))
    corner_peers = ((right, up), (right, down), (left, up), (left, down))

    y_halves = [pl.ds(0, 8), pl.ds(8, 8)]
    table = {name: (tables_h[name], tables[name]) for name in names}
    groups = [
        [(base_h.at[:, :, y_halves[e], :], b_s.at[:, e]) for e in range(2)]
        + [table[n] for n in ("xy_interp", "flow_ends", "sigma_xy", "sigma_z")]
        + [(md_h, md_s), (mc_h, mc_s)]
        + [(adj_h.at[:, :, y_halves[e], :], v_s.at[:, e]) for e in range(2)]
        + [table[n] for n in ("choose_ends", "node_weights", "to_ends", "xy_grad")],
        [table[n] for n in ("xy_grad_back", "xy_back_12", "xy_back_3", "from_ends")]
        + [(jac_h.at[:, y_halves[e], :], j_s.at[e]) for e in range(2)],
        [table[n] for n in ("z_grad", "z_grad_back", "flow_middle", "to_middle", "from_middle")],
    ]
    loads, used = [], 0
    for group in groups:
        loads.append(
            [
                pltpu.make_async_copy(source, target, load_sem.at[used + i])
                for i, (source, target) in enumerate(group)
            ]
        )
        used += len(group)
    for group in loads:
        for copy in group:
            copy.start()

    def arrive(group):
        for copy in loads[group]:
            copy.wait()

    barrier = pltpu.get_barrier_semaphore()
    for peer in x_peers + z_peers:
        pl.semaphore_signal(barrier, inc=1, device_id=peer, device_id_type=MESH)

    lanes = [slice(128 * c, 128 * c + 128) for c in range(4)]
    halves_of = [slice(0, 64), slice(64, 128)]
    lane = lax.broadcasted_iota(jnp.int32, (128, 128), 1)
    at_end = (lane < 8) | (lane >= 120)

    def on_left(name, value):
        return mm(tables[name][...], stack_rows(value))

    def pair(i, j):
        return i if i == j else 2 + i + j

    def flux_of(factor, grads):
        return [
            factor(pair(d, 0)) * grads[0]
            + factor(pair(d, 1)) * grads[1]
            + factor(pair(d, 2)) * grads[2]
            for d in range(3)
        ]

    def end_operator(field):
        packed = jnp.where(
            lane < 16,
            pltpu.roll(field[0], 8, 1),
            jnp.where(lane < 32, pltpu.roll(field[1], 24, 1), pltpu.roll(field[2], 40, 1)),
        )
        lines = mm_right(stack_lanes(packed), tables["to_ends"])
        joined = []
        planar = []
        for e in range(2):
            rows = halves_of[e]
            fine = on_left("xy_interp", lines[rows, 128:])
            grads = on_left("xy_grad", packed[rows])
            flux = flux_of(
                lambda slot: ge_s[slot, e], (grads[:64], grads[64:], lines[rows, :128])
            )
            first = jnp.concatenate([ue_s[d, e] * fine for d in range(2)], axis=0)
            back_12 = on_left("xy_back_12", first)
            back_3 = on_left("xy_back_3", ue_s[2, e] * fine)
            planar.append(on_left("xy_grad_back", jnp.concatenate(flux[:2], axis=0)))
            joined.append(jnp.concatenate([back_12, back_3, flux[2]], axis=1))
        normal = mm_right(stack_lanes(jnp.concatenate(joined, axis=0)), tables["from_ends"])
        return normal + jnp.concatenate(planar, axis=0)

    def stiffness(high, low):
        stacked = jnp.concatenate(
            [jnp.concatenate([high[c], low[c], high[c]], axis=1) for c in range(3)], axis=0
        )
        grad_z = mm_right(stacked, tables["z_grad"])
        planar, fluxes = [], [[None, None] for _ in range(3)]
        for e in range(2):
            wide_high = jnp.concatenate([high[c][halves_of[e]] for c in range(3)], axis=1)
            wide_low = jnp.concatenate([low[c][halves_of[e]] for c in range(3)], axis=1)
            grads = mm(
                tables["xy_grad"][...],
                jnp.concatenate([wide_high, wide_low, wide_high], axis=0),
            )
            flux = [[None] * 3 for _ in range(2)]
            for c in range(3):
                start = 128 * c + 64 * e
                g = (grads[:64, lanes[c]], grads[64:, lanes[c]], grad_z[start : start + 64])
                flux[0][c], flux[1][c], fluxes[c][e] = flux_of(lambda slot: gw_s[slot, e], g)
            joined = jnp.concatenate([jnp.concatenate(f, axis=1) for f in flux], axis=0)
            planar.append(on_left("xy_grad_back", joined))
        normal = mm_right(
            stack_lanes(jnp.concatenate([f for two in fluxes for f in two], axis=0)),
            tables["z_grad_back"],
        )
        return jnp.concatenate(planar, axis=0) + jnp.concatenate(
            [normal[128 * c : 128 * c + 128] for c in range(3)], axis=1
        )

    def middle_convection(field, high, low):
        shifted_high, shifted_low = split(pltpu.roll(field[2], 72, 1))
        stacked = jnp.concatenate(
            [
                jnp.concatenate([high[0], high[2], low[0], low[2], high[0], high[2]], axis=1),
                jnp.concatenate(
                    [high[1], shifted_high, low[1], shifted_low, high[1], shifted_high], axis=1
                ),
            ],
            axis=0,
        )
        both = mm_right(stacked, tables["to_middle"])
        lines = jnp.concatenate([both[:128], both[128:]], axis=1)
        pieces = []
        for e in range(2):
            fine = on_left("xy_interp", lines[halves_of[e]])

            def product(d):
                return jnp.concatenate(
                    [
                        um_s[d, e, :, lanes[k]] * fine[:, lanes[i]]
                        for i, k in enumerate((0, 1, 0, 2))
                    ],
                    axis=1,
                )

            first = jnp.concatenate([product(0), product(1)], axis=0)
            pieces.append((on_left("xy_back_12", first), on_left("xy_back_3", product(2))))
        joined = [
            jnp.concatenate([part[:, 256 * t : 256 * t + 256] for part in pieces[e]], axis=1)
            for t in range(2)
            for e in range(2)
        ]
        back = mm_right(stack_lanes(jnp.concatenate(joined, axis=0)), tables["from_middle"])
        tail = back[:128, 128:] + pltpu.roll(back[128:, 128:], 56, 1)
        return jnp.concatenate([back[:128, :128], back[128:, :128], tail], axis=1)

    def with_ends(value, end_tile):
        return jnp.concatenate(
            [
                jnp.where(at_end, pltpu.roll(end_tile, 120 - 16 * c, 1), value[:, lanes[c]])
                for c in range(3)
            ],
            axis=1,
        )

    def local_sum(value, low, high):
        width, count = value.shape[1], high - low
        two = [value[64 * e + 8 * low : 64 * e + 8 * high] for e in range(2)]
        two = [member.reshape(count, 8, width) for member in two]
        place = lax.broadcasted_iota(jnp.int32, (count, 8, width), 1)
        lane = lax.broadcasted_iota(jnp.int32, (8 * count, 128), 1)
        begins = (lane % 8 == 0) & (lane > 0)
        closes = (lane % 8 == 7) & (lane < 127)
        results = []
        for own, other in ((two[0], two[1]), (two[1], two[0])):
            before = pltpu.roll(other, 1, 1)
            after = pltpu.roll(other, 7, 1)
            total = own + jnp.where(place == 7, after, jnp.where(place == 0, before, 0.0))
            total = total.reshape(8 * count, width)
            pieces = []
            for c in range(width // 128):
                piece = total[:, lanes[c]]
                near = jnp.where(
                    closes,
                    pltpu.roll(piece, 127, 1),
                    jnp.where(begins, pltpu.roll(piece, 1, 1), 0.0),
                )
                pieces.append(piece + near)
            results.append(jnp.concatenate(pieces, axis=1))
        return results

    def picks_of(width, find):
        row = lax.broadcasted_iota(jnp.int32, (8, width), 0)
        lane = lax.broadcasted_iota(jnp.int32, (8, width), 1)
        return find(row, lane).astype(F32).astype(BF16)

    picks_in = picks_of(
        512,
        lambda row, lane: ((row < 4) & (lane == 128 * row))
        | ((row >= 4) & (lane == 128 * (row - 4) + 127)),
    )
    picks_out = picks_of(
        256,
        lambda row, lane: ((row < 3) & (lane == 16 * row + 8))
        | ((row >= 4) & (row < 7) & (lane == 16 * (row - 4) + 7))
        | ((row == 3) & (lane == 128))
        | ((row == 7) & (lane == 255)),
    )
    side = lax.broadcasted_iota(jnp.int32, (8, 128), 0)
    place = lax.broadcasted_iota(jnp.int32, (8, 128), 1) % 64

    def remote(source, target, phase, i, peer):
        return pltpu.make_async_remote_copy(
            src_ref=source,
            dst_ref=target,
            send_sem=send_sem.at[phase, i],
            recv_sem=recv_sem.at[phase, i],
            device_id=peer,
            device_id_type=MESH,
        )

    def send_ends(phase, value, extra_peers):
        high, low = split(value)
        picks = picks_out[:, : value.shape[1]]
        contract = (((1,), (1,)), ((), ()))
        tile = lax.dot_general(
            picks, high, contract, preferred_element_type=F32
        ) + lax.dot_general(picks, low, contract, preferred_element_type=F32)
        after = jnp.where(place % 8 == 7, pltpu.roll(tile, 71, 1), 0.0)
        before = jnp.where(place % 8 == 0, pltpu.roll(tile, 57, 1), 0.0)
        zs[phase] = tile + after + before
        copies = [
            remote(zs.at[phase], zr.at[phase, i], phase, 2 + i, peer)
            for i, peer in enumerate(z_peers)
        ]
        extra = [
            remote(zs.at[phase], dr.at[i], phase, 4 + i, peer)
            for i, peer in enumerate(extra_peers)
        ]
        for copy in extra + copies:
            copy.start()
        return copies, extra

    def exchange(phase, value, xs, xr, z_copies, corner_copies):
        faces = [local_sum(value, 7, 8), local_sum(value, 0, 1)]
        for i in range(2):
            for e in range(2):
                xs[i, 8 * e : 8 * e + 8] = faces[i][e]
        x_copies = [
            remote(xs.at[i], xr.at[i], phase, i, peer) for i, peer in enumerate(x_peers)
        ]
        for copy in x_copies:
            copy.start()
        inner = local_sum(value, 1, 7)
        for copy in z_copies:
            copy.wait_recv()
        from_down = (side >= 4) & (col > 0)
        from_up = (side < 4) & (col < n_col - 1)

        def choose(below, above):
            return jnp.where(from_down, below, jnp.where(from_up, above, 0.0))

        lines = choose(zr[phase, 0], zr[phase, 1])
        if corner_copies:
            others = corner_copies
        else:
            rs[...] = lines
            others = [
                remote(rs, rr.at[i], phase, 4 + i, peer) for i, peer in enumerate(x_peers)
            ]
            for copy in others:
                copy.start()
        for copy in x_copies + others:
            copy.wait_recv()
        if corner_copies:
            beside = (choose(dr[0], dr[1]), choose(dr[2], dr[3]))
        else:
            beside = (rr[0], rr[1])
        lines = lines + jnp.where(place < 8, pltpu.roll(beside[0], 72, 1), 0.0)
        lines = lines + jnp.where(place >= 56, pltpu.roll(beside[1], 56, 1), 0.0)
        lines = pltpu.roll(lines, 4, 0)
        columns = jnp.transpose(jnp.concatenate([lines] * 16, axis=0))[:, :8]
        high, low = split(columns)
        picks = picks_in[:, : value.shape[1]]
        pieces = []
        for e in range(2):
            pieces.append(faces[1][e] + xr[0, 8 * e : 8 * e + 8])
            pieces.append(inner[e])
            pieces.append(faces[0][e] + xr[1, 8 * e : 8 * e + 8])
        total = jnp.concatenate(pieces, axis=0) + (mm(high, picks) + mm(low, picks))
        for copy in x_copies + z_copies + others:
            copy.wait_send()
        return total

    lane_row = lax.broadcasted_iota(jnp.int32, (1, 128), 1)
    wall = ((lane_row == 0) & (col == 0)) | ((lane_row == 127) & (col == n_col - 1))
    interior = jnp.where(wall, 0.0, 1.0).astype(F32)

    arrive(0)
    fine_rows = []
    for e in range(2):
        rows = jnp.concatenate([b_s[d, e].reshape(64, 128) for d in range(3)], axis=1)
        fine = on_left("xy_interp", rows)
        fine_rows.extend(fine[:, lanes[d]] for d in range(3))
    fine_rows = stack_lanes(jnp.concatenate(fine_rows, axis=0))
    fine_weights = tables["sigma_xy"][:, :1] * tables["sigma_z"][:1]
    flow = mm_right(fine_rows, tables["flow_ends"])
    for e in range(2):
        for d in range(3):
            first = 144 * (3 * e + d)
            ue_s[d, e] = flow[first : first + 144] * fine_weights[:, lanes[0]]

    weights = VISCOSITY * tables["node_weights"][...]
    end_weights = jnp.where(
        lane[:64] < 16,
        pltpu.roll(weights, 8, 1),
        jnp.where(lane[:64] < 32, pltpu.roll(weights, 24, 1), pltpu.roll(weights, 40, 1)),
    )
    factors = []
    for name in (md_s, mc_s):
        for i in range(3):
            plane = name[i].astype(F32)
            for e in range(2):
                factors.append(plane[:, 8 * e : 8 * e + 8, :].reshape(64, 128))
    end_factors = mm(
        jnp.concatenate(factors, axis=0).astype(BF16), tables["choose_ends"][...]
    )
    for i, factor in enumerate(factors):
        ge_s[i // 2, i % 2] = end_factors[64 * i : 64 * i + 64] * end_weights
        gw_s[i // 2, i % 2] = factor * weights

    start = [v_s[c].reshape(128, 128) for c in range(3)]
    arrive(1)
    end_tile = end_operator(start)
    mass = jnp.concatenate(
        [j_s[e].reshape(64, 128) * tables["node_weights"][...] for e in range(2)], axis=0
    )
    pl.semaphore_wait(barrier, 4)
    z_copies, corner_copies = send_ends(0, jnp.concatenate([end_tile, mass], axis=1), ())

    arrive(2)
    flow = mm_right(fine_rows, tables["flow_middle"])
    for e in range(2):
        for d in range(3):
            first = 144 * (3 * e + d)
            um_s[d, e] = flow[first : first + 144] * fine_weights[:, 128:]

    pairs = [split(member) for member in start]
    high, low = [p[0] for p in pairs], [p[1] for p in pairs]
    value = middle_convection(start, high, low) + stiffness(high, low)
    value = jnp.concatenate([with_ends(value, end_tile), mass], axis=1)
    total = exchange(0, value, xs0, xr0, z_copies, corner_copies)
    inverse = 1.0 / total[:, lanes[3]]
    half = [
        interior * (start[c] - (0.5 * STEP_SIZE) * inverse * total[:, lanes[c]]) for c in range(3)
    ]

    end_tile = end_operator(half)
    z_copies, corner_copies = send_ends(1, end_tile, corner_peers)
    pairs = [split(member) for member in half]
    high, low = [p[0] for p in pairs], [p[1] for p in pairs]
    value = middle_convection(half, high, low) + stiffness(high, low)
    value = with_ends(value, end_tile)
    total = exchange(1, value, xs1, xr1, z_copies, corner_copies)
    for c in range(3):
        result = interior * (
            v_s[c].reshape(128, 128) - STEP_SIZE * inverse * total[:, lanes[c]]
        )
        for e in range(2):
            out[c, :, 8 * e : 8 * e + 8, :] = result[halves_of[e]].reshape(8, 8, 128)


def local(n_span, n_col, adjoint_field, base_flow, metric_diag, metric_cross, jacobian):
    tables = operator_tables()
    table_scratch = [
        pltpu.VMEM(member.shape, jnp.dtype(member.dtype)) for member in tables.values()
    ]
    return pl.pallas_call(
        functools.partial(kernel, n_span, n_col, tuple(tables)),
        out_shape=pltpu.VMEM(adjoint_field.shape, F32),
        in_specs=[pl.BlockSpec(memory_space=pl.ANY)] * (5 + len(tables)),
        out_specs=pl.BlockSpec(memory_space=pltpu.VMEM),
        scratch_shapes=[
            pltpu.VMEM((3, 2, 8, 8, 128), F32),
            pltpu.VMEM((3, 2, 8, 8, 128), F32),
            pltpu.VMEM((2, 8, 8, 128), F32),
            pltpu.VMEM((3, 8, 16, 128), BF16),
            pltpu.VMEM((3, 8, 16, 128), BF16),
            *table_scratch,
            pltpu.VMEM((3, 2, 144, 128), F32),
            pltpu.VMEM((3, 2, 144, 384), F32),
            pltpu.VMEM((6, 2, 64, 128), F32),
            pltpu.VMEM((6, 2, 64, 128), F32),
            pltpu.VMEM((2, 16, 512), F32),
            pltpu.VMEM((2, 16, 512), F32),
            pltpu.VMEM((2, 16, 384), F32),
            pltpu.VMEM((2, 16, 384), F32),
            pltpu.VMEM((2, 8, 128), F32),
            pltpu.VMEM((2, 2, 8, 128), F32),
            pltpu.VMEM((8, 128), F32),
            pltpu.VMEM((2, 8, 128), F32),
            pltpu.VMEM((4, 8, 128), F32),
            pltpu.SemaphoreType.DMA((8 + len(tables),)),
            pltpu.SemaphoreType.DMA((2, 8)),
            pltpu.SemaphoreType.DMA((2, 8)),
        ],
        compiler_params=pltpu.CompilerParams(collective_id=0, has_side_effects=True),
    )(
        adjoint_field,
        base_flow,
        metric_diag,
        metric_cross,
        jacobian,
        *[jnp.asarray(member) for member in tables.values()],
    )


def solution(mesh):
    in_specs = (
        P(None, "span", None, "col"),
        P(None, "span", None, "col"),
        P(None, "span", None, "col"),
        P(None, "span", None, "col"),
        P("span", None, "col"),
    )
    out_specs = P(None, "span", None, "col")
    body = functools.partial(local, mesh.shape["span"], mesh.shape["col"])
    return jax.shard_map(body, mesh=mesh, in_specs=in_specs, out_specs=out_specs, check_vma=False)
```

time: 36.6 us -> 35.3 us (0.964)
  Pallas kernels: 35.8 us -> 34.5 us
    pallas_call x1, Pallas kernels: 35.8 us -> 34.5 us  [local(): pl.pallas_call(functools.partial(kernel, n_span, n_col, tuple(tables)), o...]
where the time goes in v3:
time: 35.3 us; the launch traced here: 35.2 us
  Pallas kernels  34.5 us (98%)
  local copies, waits for them, and re-layouts  0.68 us (2%)
    pallas_call x1, Pallas kernels, local(): pl.pallas_call(functools.partial(kernel, n_span, n_col, tuple(tables)), o...  34.5 us

profile of v3, /device:TPU:1, one launch (start us, length us, event | category | flops | bytes accessed | tf_op | source)
XLA Modules:
  0.0 35.2 jit_solution(17593361855054209529)
XLA Ops:
  0.0 34.5 %shard_map.208 = f32[3,8,16,128]{3,2,1,0:T(8,128)S(1)} custom-call(f32[3,8,16,128]{3,2,1,0:T(8,128)} %refs_0_.1, f32[3,8,16,128]{3,2,1,0:T(8,128)} %refs_1_.1, bf16[3,8,16,128]{3,2,1,0:T(8,128)(2,1)} %refs_2_.1, bf16[3,8,16,128]{3,2,1,0:T(8,128)(2,1)} %refs_3_.1, f32[8,16,128]{2,1,0:T(8,128)} %refs_4_.1, bf16[2,128,128]{2,1,0:T(8,128)(2,1)} %constant.34.clone.refs_5_, ...), custom_call_target="tpu_custom_call" | custom-call | tf_op jit(solution)/shard_map/pallas_call | solution.py:586
  34.5 0.7 %copy.24 = f32[3,8,16,128]{3,2,1,0:T(8,128)} copy(f32[3,8,16,128]{3,2,1,0:T(8,128)S(1)} %shard_map.208) | data formatting | bytes 393216

commit v4 on v3

--- a/solution.py
+++ b/solution.py
@@ -210,27 +210,25 @@
     (v_s, b_s, j_s, md_s, mc_s) = refs[:5]
     tables = dict(zip(names, refs[5 : 5 + n_tables]))
     refs = refs[5 + n_tables :]
-    (ue_s, um_s, ge_s, gw_s, xs0, xr0, xs1, xr1, zs, zr, rs, rr, dr) = refs[:13]
-    (load_sem, send_sem, recv_sem) = refs[13:]
+    (ue_s, um_s, ge_s, gw_s, xs0, xr0, xs1, xr1, zs, zr, cr) = refs[:11]
+    (load_sem, send_sem, recv_sem) = refs[11:]
 
     span = lax.axis_index("span")
     col = lax.axis_index("col")
     right, left = lax.rem(span + 1, n_span), lax.rem(span + n_span - 1, n_span)
     up, down = lax.rem(col + 1, n_col), lax.rem(col + n_col - 1, n_col)
     x_peers = ((right, col), (left, col))
-    z_peers = ((span, up), (span, down))
-    corner_peers = ((right, up), (right, down), (left, up), (left, down))
-
-    y_halves = [pl.ds(0, 8), pl.ds(8, 8)]
+    has_up, has_down = col < n_col - 1, col > 0
+
     table = {name: (tables_h[name], tables[name]) for name in names}
     groups = [
-        [(base_h.at[:, :, y_halves[e], :], b_s.at[:, e]) for e in range(2)]
+        [(base_h, b_s)]
         + [table[n] for n in ("xy_interp", "flow_ends", "sigma_xy", "sigma_z")]
         + [(md_h, md_s), (mc_h, mc_s)]
-        + [(adj_h.at[:, :, y_halves[e], :], v_s.at[:, e]) for e in range(2)]
+        + [(adj_h, v_s)]
         + [table[n] for n in ("choose_ends", "node_weights", "to_ends", "xy_grad")],
         [table[n] for n in ("xy_grad_back", "xy_back_12", "xy_back_3", "from_ends")]
-        + [(jac_h.at[:, y_halves[e], :], j_s.at[e]) for e in range(2)],
+        + [(jac_h, j_s)],
         [table[n] for n in ("z_grad", "z_grad_back", "flow_middle", "to_middle", "from_middle")],
     ]
     loads, used = [], 0
@@ -251,8 +249,19 @@
             copy.wait()
 
     barrier = pltpu.get_barrier_semaphore()
-    for peer in x_peers + z_peers:
-        pl.semaphore_signal(barrier, inc=1, device_id=peer, device_id_type=MESH)
+
+    def greet(peers):
+        for peer in peers:
+            pl.semaphore_signal(barrier, inc=1, device_id=peer, device_id_type=MESH)
+
+    greet(x_peers)
+    pl.when(has_up)(lambda: greet(((span, up), (right, up))))
+    pl.when(has_down)(lambda: greet(((span, down), (left, down))))
+
+    def await_peers():
+        inside = has_up & has_down
+        pl.when(inside)(lambda: pl.semaphore_wait(barrier, 6))
+        pl.when(jnp.logical_not(inside))(lambda: pl.semaphore_wait(barrier, 4))
 
     lanes = [slice(128 * c, 128 * c + 128) for c in range(4)]
     halves_of = [slice(0, 64), slice(64, 128)]
@@ -402,11 +411,6 @@
         lane = lax.broadcasted_iota(jnp.int32, (8, width), 1)
         return find(row, lane).astype(F32).astype(BF16)
 
-    picks_in = picks_of(
-        512,
-        lambda row, lane: ((row < 4) & (lane == 128 * row))
-        | ((row >= 4) & (lane == 128 * (row - 4) + 127)),
-    )
     picks_out = picks_of(
         256,
         lambda row, lane: ((row < 3) & (lane == 16 * row + 8))
@@ -427,7 +431,7 @@
             device_id_type=MESH,
         )
 
-    def send_ends(phase, value, extra_peers):
+    def send_ends(phase, value):
         high, low = split(value)
         picks = picks_out[:, : value.shape[1]]
         contract = (((1,), (1,)), ((), ()))
@@ -437,19 +441,25 @@
         after = jnp.where(place % 8 == 7, pltpu.roll(tile, 71, 1), 0.0)
         before = jnp.where(place % 8 == 0, pltpu.roll(tile, 57, 1), 0.0)
         zs[phase] = tile + after + before
+        tile = zs.at[phase]
         copies = [
-            remote(zs.at[phase], zr.at[phase, i], phase, 2 + i, peer)
-            for i, peer in enumerate(z_peers)
+            (remote(tile, zr.at[phase, 0], phase, 2, (span, up)), has_up, has_down),
+            (remote(tile, zr.at[phase, 1], phase, 3, (span, down)), has_down, has_up),
+            (remote(tile, cr.at[phase, 0], phase, 4, (right, up)), has_up, has_down),
+            (remote(tile, cr.at[phase, 3], phase, 7, (left, down)), has_down, has_up),
         ]
-        extra = [
-            remote(zs.at[phase], dr.at[i], phase, 4 + i, peer)
-            for i, peer in enumerate(extra_peers)
-        ]
-        for copy in extra + copies:
-            copy.start()
-        return copies, extra
-
-    def exchange(phase, value, xs, xr, z_copies, corner_copies):
+        if phase == 1:
+            copies += [
+                (remote(tile, cr.at[phase, 1], phase, 5, (right, down)), has_down, has_up),
+                (remote(tile, cr.at[phase, 2], phase, 6, (left, up)), has_up, has_down),
+            ]
+        for copy, sends, _ in copies:
+            pl.when(sends)(copy.start)
+        return copies
+
+    sent = []
+
+    def exchange(phase, value, xs, xr, copies):
         faces = [local_sum(value, 7, 8), local_sum(value, 0, 1)]
         for i in range(2):
             for e in range(2):
@@ -460,44 +470,56 @@
         for copy in x_copies:
             copy.start()
         inner = local_sum(value, 1, 7)
-        for copy in z_copies:
+        if phase == 0:
+            relays = [
+                (remote(zr.at[0, 1], cr.at[0, 1], 0, 5, (right, col)), has_up, has_up),
+                (remote(zr.at[0, 0], cr.at[0, 2], 0, 6, (left, col)), has_down, has_down),
+            ]
+            def forward(order):
+                for k in order:
+                    pl.when(copies[1 - k][2])(copies[1 - k][0].wait_recv)
+                    pl.when(relays[k][1])(relays[k][0].start)
+
+            pl.when(col % 2 == 0)(lambda: forward((0, 1)))
+            pl.when(col % 2 == 1)(lambda: forward((1, 0)))
+            pending = copies[2:] + relays
+            all_copies = copies + relays
+        else:
+            pending = all_copies = copies
+        for copy, _, receives in pending:
+            pl.when(receives)(copy.wait_recv)
+        for copy in x_copies:
             copy.wait_recv()
-        from_down = (side >= 4) & (col > 0)
-        from_up = (side < 4) & (col < n_col - 1)
+        from_down = (side >= 4) & has_down
+        from_up = (side < 4) & has_up
 
         def choose(below, above):
             return jnp.where(from_down, below, jnp.where(from_up, above, 0.0))
 
         lines = choose(zr[phase, 0], zr[phase, 1])
-        if corner_copies:
-            others = corner_copies
-        else:
-            rs[...] = lines
-            others = [
-                remote(rs, rr.at[i], phase, 4 + i, peer) for i, peer in enumerate(x_peers)
-            ]
-            for copy in others:
-                copy.start()
-        for copy in x_copies + others:
-            copy.wait_recv()
-        if corner_copies:
-            beside = (choose(dr[0], dr[1]), choose(dr[2], dr[3]))
-        else:
-            beside = (rr[0], rr[1])
+        beside = (choose(cr[phase, 0], cr[phase, 1]), choose(cr[phase, 2], cr[phase, 3]))
         lines = lines + jnp.where(place < 8, pltpu.roll(beside[0], 72, 1), 0.0)
         lines = lines + jnp.where(place >= 56, pltpu.roll(beside[1], 56, 1), 0.0)
         lines = pltpu.roll(lines, 4, 0)
-        columns = jnp.transpose(jnp.concatenate([lines] * 16, axis=0))[:, :8]
-        high, low = split(columns)
-        picks = picks_in[:, : value.shape[1]]
+        columns = jnp.transpose(lines)
+        added = jnp.concatenate(
+            [
+                jnp.where(
+                    lane == 0,
+                    columns[:, c : c + 1],
+                    jnp.where(lane == 127, columns[:, 4 + c : 5 + c], 0.0),
+                )
+                for c in range(value.shape[1] // 128)
+            ],
+            axis=1,
+        )
         pieces = []
         for e in range(2):
             pieces.append(faces[1][e] + xr[0, 8 * e : 8 * e + 8])
             pieces.append(inner[e])
             pieces.append(faces[0][e] + xr[1, 8 * e : 8 * e + 8])
-        total = jnp.concatenate(pieces, axis=0) + (mm(high, picks) + mm(low, picks))
-        for copy in x_copies + z_copies + others:
-            copy.wait_send()
+        total = jnp.concatenate(pieces, axis=0) + added
+        sent.extend([(copy, True) for copy in x_copies] + [c[:2] for c in all_copies])
         return total
 
     lane_row = lax.broadcasted_iota(jnp.int32, (1, 128), 1)
@@ -507,7 +529,7 @@
     arrive(0)
     fine_rows = []
     for e in range(2):
-        rows = jnp.concatenate([b_s[d, e].reshape(64, 128) for d in range(3)], axis=1)
+        rows = jnp.concatenate([b_s[d, :, 8 * e : 8 * e + 8, :].reshape(64, 128) for d in range(3)], axis=1)
         fine = on_left("xy_interp", rows)
         fine_rows.extend(fine[:, lanes[d]] for d in range(3))
     fine_rows = stack_lanes(jnp.concatenate(fine_rows, axis=0))
@@ -537,14 +559,17 @@
         ge_s[i // 2, i % 2] = end_factors[64 * i : 64 * i + 64] * end_weights
         gw_s[i // 2, i % 2] = factor * weights
 
-    start = [v_s[c].reshape(128, 128) for c in range(3)]
+    def field_of(c):
+        return jnp.concatenate(
+            [v_s[c, :, 8 * e : 8 * e + 8, :].reshape(64, 128) for e in range(2)], axis=0
+        )
+
+    start = [field_of(c) for c in range(3)]
     arrive(1)
     end_tile = end_operator(start)
     mass = jnp.concatenate(
-        [j_s[e].reshape(64, 128) * tables["node_weights"][...] for e in range(2)], axis=0
-    )
-    pl.semaphore_wait(barrier, 4)
-    z_copies, corner_copies = send_ends(0, jnp.concatenate([end_tile, mass], axis=1), ())
+        [j_s[:, 8 * e : 8 * e + 8, :].reshape(64, 128) * tables["node_weights"][...] for e in range(2)], axis=0
+    )
 
     arrive(2)
     flow = mm_right(fine_rows, tables["flow_middle"])
@@ -555,27 +580,35 @@
 
     pairs = [split(member) for member in start]
     high, low = [p[0] for p in pairs], [p[1] for p in pairs]
-    value = middle_convection(start, high, low) + stiffness(high, low)
+    value = middle_convection(start, high, low)
+    value = value + stiffness(high, low)
+    await_peers()
+    copies = send_ends(0, jnp.concatenate([end_tile, mass], axis=1))
     value = jnp.concatenate([with_ends(value, end_tile), mass], axis=1)
-    total = exchange(0, value, xs0, xr0, z_copies, corner_copies)
+    total = exchange(0, value, xs0, xr0, copies)
     inverse = 1.0 / total[:, lanes[3]]
     half = [
         interior * (start[c] - (0.5 * STEP_SIZE) * inverse * total[:, lanes[c]]) for c in range(3)
     ]
 
     end_tile = end_operator(half)
-    z_copies, corner_copies = send_ends(1, end_tile, corner_peers)
+    copies = send_ends(1, end_tile)
     pairs = [split(member) for member in half]
     high, low = [p[0] for p in pairs], [p[1] for p in pairs]
     value = middle_convection(half, high, low) + stiffness(high, low)
     value = with_ends(value, end_tile)
-    total = exchange(1, value, xs1, xr1, z_copies, corner_copies)
+    total = exchange(1, value, xs1, xr1, copies)
     for c in range(3):
         result = interior * (
-            v_s[c].reshape(128, 128) - STEP_SIZE * inverse * total[:, lanes[c]]
+            field_of(c) - STEP_SIZE * inverse * total[:, lanes[c]]
         )
         for e in range(2):
             out[c, :, 8 * e : 8 * e + 8, :] = result[halves_of[e]].reshape(8, 8, 128)
+    for copy, sends in sent:
+        if sends is True:
+            copy.wait_send()
+        else:
+            pl.when(sends)(copy.wait_send)
 
 
 def local(n_span, n_col, adjoint_field, base_flow, metric_diag, metric_cross, jacobian):
@@ -589,9 +622,9 @@
         in_specs=[pl.BlockSpec(memory_space=pl.ANY)] * (5 + len(tables)),
         out_specs=pl.BlockSpec(memory_space=pltpu.VMEM),
         scratch_shapes=[
-            pltpu.VMEM((3, 2, 8, 8, 128), F32),
-            pltpu.VMEM((3, 2, 8, 8, 128), F32),
-            pltpu.VMEM((2, 8, 8, 128), F32),
+            pltpu.VMEM((3, 8, 16, 128), F32),
+            pltpu.VMEM((3, 8, 16, 128), F32),
+            pltpu.VMEM((8, 16, 128), F32),
             pltpu.VMEM((3, 8, 16, 128), BF16),
             pltpu.VMEM((3, 8, 16, 128), BF16),
             *table_scratch,
@@ -605,10 +638,8 @@
             pltpu.VMEM((2, 16, 384), F32),
             pltpu.VMEM((2, 8, 128), F32),
             pltpu.VMEM((2, 2, 8, 128), F32),
-            pltpu.VMEM((8, 128), F32),
-            pltpu.VMEM((2, 8, 128), F32),
-            pltpu.VMEM((4, 8, 128), F32),
-            pltpu.SemaphoreType.DMA((8 + len(tables),)),
+            pltpu.VMEM((2, 4, 8, 128), F32),
+            pltpu.SemaphoreType.DMA((5 + len(tables),)),
             pltpu.SemaphoreType.DMA((2, 8)),
             pltpu.SemaphoreType.DMA((2, 8)),
         ],

time: 35.3 us -> 33.2 us (0.941)
  Pallas kernels: 34.5 us -> 32.4 us
    pallas_call x1, Pallas kernels: 34.5 us -> 32.4 us  [local(): pl.pallas_call(functools.partial(kernel, n_span, n_col, tuple(tables)), o...]
where the time goes in v4:
time: 33.2 us; the launch traced here: 33.1 us
  Pallas kernels  32.4 us (98%)
  local copies, waits for them, and re-layouts  0.68 us (2%)
    pallas_call x1, Pallas kernels, local(): pl.pallas_call(functools.partial(kernel, n_span, n_col, tuple(tables)), o...  32.4 us
    unnamed x1, local copies, waits for them, and re-layouts  0.68 us

profile of v4, /device:TPU:1, one launch (start us, length us, event | category | flops | bytes accessed | tf_op | source)
XLA Modules:
  0.0 33.1 jit_solution(7561398662855387833)
XLA Ops:
  0.0 32.4 %shard_map.208 = f32[3,8,16,128]{3,2,1,0:T(8,128)S(1)} custom-call(f32[3,8,16,128]{3,2,1,0:T(8,128)} %refs_0_.1, f32[3,8,16,128]{3,2,1,0:T(8,128)} %refs_1_.1, bf16[3,8,16,128]{3,2,1,0:T(8,128)(2,1)} %refs_2_.1, bf16[3,8,16,128]{3,2,1,0:T(8,128)(2,1)} %refs_3_.1, f32[8,16,128]{2,1,0:T(8,128)} %refs_4_.1, bf16[2,128,128]{2,1,0:T(8,128)(2,1)} %constant.34.clone.refs_5_, ...), custom_call_target="tpu_custom_call" | custom-call | tf_op jit(solution)/shard_map/pallas_call | solution.py:619
  32.4 0.7 %copy.24 = f32[3,8,16,128]{3,2,1,0:T(8,128)} copy(f32[3,8,16,128]{3,2,1,0:T(8,128)S(1)} %shard_map.208) | data formatting | bytes 393216

commit v5 on v4

--- a/solution.py
+++ b/solution.py
@@ -566,7 +566,6 @@
 
     start = [field_of(c) for c in range(3)]
     arrive(1)
-    end_tile = end_operator(start)
     mass = jnp.concatenate(
         [j_s[:, 8 * e : 8 * e + 8, :].reshape(64, 128) * tables["node_weights"][...] for e in range(2)], axis=0
     )
@@ -581,6 +580,7 @@
     pairs = [split(member) for member in start]
     high, low = [p[0] for p in pairs], [p[1] for p in pairs]
     value = middle_convection(start, high, low)
+    end_tile = end_operator(start)
     value = value + stiffness(high, low)
     await_peers()
     copies = send_ends(0, jnp.concatenate([end_tile, mass], axis=1))

time: 33.2 us -> 33.2 us (level)
  no operation moved by 1% of the time
where the time goes in v5:
time: 33.2 us; the launch traced here: 33 us
  Pallas kernels  32.3 us (97%)
  local copies, waits for them, and re-layouts  0.68 us (2%)
    pallas_call x1, Pallas kernels, local(): pl.pallas_call(functools.partial(kernel, n_span, n_col, tuple(tables)), o...  32.3 us
    unnamed x1, local copies, waits for them, and re-layouts  0.68 us

profile of v5, /device:TPU:1, one launch (start us, length us, event | category | flops | bytes accessed | tf_op | source)
XLA Modules:
  0.0 33.0 jit_solution(17845267379963092940)
XLA Ops:
  0.0 32.3 %shard_map.208 = f32[3,8,16,128]{3,2,1,0:T(8,128)S(1)} custom-call(f32[3,8,16,128]{3,2,1,0:T(8,128)} %refs_0_.1, f32[3,8,16,128]{3,2,1,0:T(8,128)} %refs_1_.1, bf16[3,8,16,128]{3,2,1,0:T(8,128)(2,1)} %refs_2_.1, bf16[3,8,16,128]{3,2,1,0:T(8,128)(2,1)} %refs_3_.1, f32[8,16,128]{2,1,0:T(8,128)} %refs_4_.1, bf16[2,128,128]{2,1,0:T(8,128)(2,1)} %constant.34.clone.refs_5_, ...), custom_call_target="tpu_custom_call" | custom-call | tf_op jit(solution)/shard_map/pallas_call | solution.py:619
  32.3 0.7 %copy.24 = f32[3,8,16,128]{3,2,1,0:T(8,128)} copy(f32[3,8,16,128]{3,2,1,0:T(8,128)S(1)} %shard_map.208) | data formatting | bytes 393216
